TPU v7x, 128 devices: a whole 4x4x4 slice. The times are simulated.
128 devices in a mesh: stn: 16 (over x_hi, z, core), freq: 8 (over x_lo, y).
Axes of the slice: x: 4 (x_hi: 2, x_lo: 2; x = x_hi * 2 + x_lo), y: 4, z: 4, core: 2. Of those that a mesh axis runs over, the one named last changes fastest.
Arguments:
- propagator: bfloat16 [48, 2000, 2000], P('stn'), may hold values from -0.125 to 0.125
- forcing: bfloat16 [48, 2, 512, 2000], P('stn', None, 'freq'), may hold values from -6 to 6
- forward: bfloat16 [48, 2, 512, 2000], P('stn', None, 'freq'), may hold values from -6 to 6
- damping: float32 [2000], replicated, may hold values from 0.0005 to 0.05
- slowness: float32 [2000], replicated, may hold values from 0.5 to 2
- station_gap: int32 [48], P('stn'), may hold values from 1 to 3
- freq_index: int32 [512], P('freq'), may hold values from 0 to 511, each once
Outputs:
- sensitivity: float32 [48, 2000], P('stn', 'freq')
Inputs may be any that keep to these rules, and one draw needn't show every extreme that they name: `freq_index`: each index of the list appears exactly once.
All inputs are finite; a program needn't handle non-finite values.
Results may differ from a plain program's by a relative error of at most 0.018.
Values may be sent and summed in bfloat16 or wider, within the bound.
No kernel may reach another device: no remote copies, remote signals or barrier semaphores. Data moves between devices by JAX's collectives and lax.ppermute only.
A program may use at most 128 MiB of HBM per device.

v0:
```python
import functools
import math

import jax
import jax.numpy as jnp
from jax import lax
from jax.experimental import pallas as pl
from jax.experimental.pallas import tpu as pltpu
from jax.sharding import PartitionSpec as P

NVAR = 5
BLOCKS = 2
PASS_ROWS = 128
TILE = 256
UNITS = 2
LANES = 128

frequency_step = 0.05

ON_CHIP = pl.BlockSpec(memory_space=pltpu.VMEM)
IN_PLACE = pl.BlockSpec(memory_space=pl.ANY)
SCALARS = pl.BlockSpec(memory_space=pltpu.SMEM)


def from_behind(value, axis, by):
    length = lax.axis_size(axis)
    pairs = [(i, i + by) for i in range(length) if 0 <= i + by < length]
    return lax.ppermute(value, axis, pairs)


def in_blocks(value, dim, length):
    dims = value.shape
    tiles = value.reshape(*dims[:dim], length, dims[dim] // length, *dims[dim + 1 :])
    return jnp.moveaxis(tiles, dim, 0)


def summed_on_arrival(value, axis, dim):
    length = lax.axis_size(axis)
    tiles = lax.all_to_all(in_blocks(value, dim, length), axis, 0, 0, tiled=True)
    return jnp.sum(tiles, axis=0)


def prepare_kernel(
    gap_hbm, freq_index_hbm, forward_hbm, damping_hbm, slowness_hbm,
    cosine, sine, slope, edge,
    angle, wide, gap, freq_index, forward, damping, slowness, arrived,
):
    stations, _, freqs, width = forward.shape
    padded = wide.shape[1]
    fetches = [
        pltpu.make_async_copy(source, target, arrived.at[i])
        for i, (source, target) in enumerate((
            (freq_index_hbm, freq_index), (slowness_hbm, slowness), (damping_hbm, damping),
            (gap_hbm, gap), (forward_hbm, forward),
        ))
    ]
    for fetch in fetches:
        fetch.start()
    wide[...] = jnp.zeros_like(wide)
    for fetch in fetches[:4]:
        fetch.wait()
    slow = slowness[...]
    for row in range(freqs):
        frequency = frequency_step * (freq_index[row].astype(jnp.float32) + 1.0)
        angle[row : row + 1, :] = frequency * slow
    damped = jnp.exp(-damping[...])
    c1 = damped * jnp.cos(angle[...])
    s1 = damped * jnp.sin(angle[...])
    wall = width // NVAR
    place = lax.rem(lax.broadcasted_iota(jnp.int32, (freqs, padded), 1), wall)
    has_next = place != wall - 1
    has_last = place != 0
    fetches[4].wait()
    edge[...] = forward[0]
    for station in range(stations):
        gap_here = gap[station]
        c2 = c1 * c1 - s1 * s1
        s2 = 2.0 * (c1 * s1)
        c3 = c2 * c1 - s2 * s1
        s3 = c2 * s1 + s2 * c1
        cosine[station] = jnp.where(gap_here == 1, c1, jnp.where(gap_here == 2, c2, c3))
        sine[station] = jnp.where(gap_here == 1, s1, jnp.where(gap_here == 2, s2, s3))
        spacing = gap_here.astype(jnp.float32)
        for part in range(2):
            here = forward[station, part].astype(jnp.float32)
            wide[:, :width] = here
            profile = wide[...]
            up = jnp.where(has_next, pltpu.roll(profile, padded - 1, 1), 0.0)
            down = jnp.where(has_last, pltpu.roll(profile, 1, 1), 0.0)
            normal = (0.5 * (up - down))[:, :width]
            if station + 1 < stations:
                after = forward[station + 1, part].astype(jnp.float32)
                slope[station, part] = (after - here) / spacing + normal
            else:
                slope[station, part] = normal - here / spacing


def prepare(gap, freq_index, forward, damping, slowness):
    stations, parts, freqs, width = forward.shape
    padded = -(-width // LANES) * LANES
    return pl.pallas_call(
        prepare_kernel,
        out_shape=(
            pltpu.VMEM((stations, freqs, width), jnp.float32),
            pltpu.VMEM((stations, freqs, width), jnp.float32),
            pltpu.VMEM((stations, parts, freqs, width), jnp.float32),
            jax.ShapeDtypeStruct((parts, freqs, width), forward.dtype),
        ),
        in_specs=[IN_PLACE] * 5,
        out_specs=(ON_CHIP,) * 4,
        scratch_shapes=[
            pltpu.VMEM((freqs, width), jnp.float32),
            pltpu.VMEM((freqs, padded), jnp.float32),
            pltpu.SMEM(gap.shape, gap.dtype),
            pltpu.SMEM(freq_index.shape, freq_index.dtype),
            pltpu.VMEM(forward.shape, forward.dtype),
            pltpu.VMEM(damping.shape, damping.dtype),
            pltpu.VMEM(slowness.shape, slowness.dtype),
            pltpu.SemaphoreType.DMA((5,)),
        ],
        cost_estimate=pl.CostEstimate(flops=16 << 30, bytes_accessed=64 << 20, transcendentals=0),
        compiler_params=pltpu.CompilerParams(vmem_limit_bytes=10 << 20),
        name="prepare",
    )(*[pltpu.with_memory_space_constraint(v, pltpu.HBM) for v in (gap, freq_index, forward, damping, slowness)])


def finish_kernel(gap, rim, slope_in, after, slope):
    del slope_in, after
    stations, parts, _, _ = slope.shape
    spacing = gap[stations - 1].astype(jnp.float32)
    for part in range(parts):
        slope[stations - 1, part] += rim[part].astype(jnp.float32) / spacing


def finish(gap, rim, slope, after):
    return pl.pallas_call(
        finish_kernel,
        out_shape=pltpu.VMEM(slope.shape, slope.dtype),
        in_specs=[SCALARS, ON_CHIP, ON_CHIP, IN_PLACE],
        out_specs=ON_CHIP,
        input_output_aliases={2: 0},
        compiler_params=pltpu.CompilerParams(vmem_limit_bytes=4 << 20),
        name="finish",
    )(gap, rim, pltpu.with_memory_space_constraint(slope, pltpu.VMEM), after)


def march_kernel(
    turn, block, first, incoming, operator, cosine, sine, forcing, slope, sums_in, *results,
):
    sums, outgoing, rows = results[0], results[1:-1], results[-1]
    stations, freqs, width = cosine.shape
    half = incoming.shape[0] // 2
    count = 2 * half
    low = block * half
    full = width // TILE
    rest = width - full * TILE
    tiles = full + 1
    groups = tiles // UNITS
    edge = width // LANES * LANES

    def settle(station, tile, mixed):
        start = tile * TILE
        size = min(TILE, width - start)
        cut = slice(start, start + size)
        real_part = forcing[station, 0, low : low + half, cut].astype(jnp.float32)
        imag_part = forcing[station, 1, low : low + half, cut].astype(jnp.float32)
        if mixed is not None:
            mixed_re, mixed_im = mixed[:half, :size], mixed[half:count, :size]
            c = cosine[station, low : low + half, cut]
            s = sine[station, low : low + half, cut]
            real_part = c * mixed_re + s * mixed_im + real_part
            imag_part = c * mixed_im - s * mixed_re + imag_part
        rows[:half, cut] = real_part.astype(jnp.bfloat16)
        rows[half:count, cut] = imag_part.astype(jnp.bfloat16)
        product = (
            real_part * slope[station, 0, low : low + half, cut]
            + imag_part * slope[station, 1, low : low + half, cut]
        )
        total = jnp.sum(product, axis=0, keepdims=True)
        if block > 0:
            total = total + sums_in[pl.ds(station, 1), cut]
        sums[pl.ds(station, 1), cut] = total

    def run(*sums_of):
        def one(step, carried):
            station = stations - 1 - step

            def piece(depth, tile):
                deep = slice(full * TILE, width)
                if not (isinstance(depth, int) and depth == full):
                    deep = pl.ds(pl.multiple_of(depth * TILE, TILE), TILE)
                cut = slice(tile * TILE, min((tile + 1) * TILE, width))
                value = operator[station, deep, cut]
                if value.shape[1] < TILE:
                    blank = jnp.zeros((value.shape[0], TILE - rest), value.dtype)
                    value = jnp.concatenate([value, blank], axis=1)
                if value.shape[0] < TILE:
                    blank = jnp.zeros((TILE - rest, TILE), value.dtype)
                    value = jnp.concatenate([value, blank], axis=0)
                return value

            def push(depth, group):
                for unit in range(UNITS):
                    pltpu.matmul_push_rhs(piece(depth, UNITS * group + unit), group % 2, unit)

            def state_at(depth):
                return rows[:, pl.ds(pl.multiple_of(depth * TILE, TILE), TILE)]

            def accumulate(state, group):
                for unit in range(UNITS):
                    pltpu.matmul_acc_lhs(sums_of[UNITS * group + unit], state, load_staged_rhs=group % 2)

            def deepen(depth, carried):
                state = state_at(depth)
                for group in range(groups):
                    if group + 1 < groups:
                        push(depth, group + 1)
                    else:
                        push(depth + 1, 0)
                    accumulate(state, group)
                return carried

            push(0, 0)
            lax.fori_loop(0, full - 1, deepen, 0)
            deepen(full - 1, 0)
            state = rows[:, full * TILE :]
            for group in range(groups):
                if group + 1 < groups:
                    push(full, group + 1)
                accumulate(state, group)
            for tile in range(tiles):
                settle(station, tile, pltpu.matmul_pop(sums_of[tile]))
            return carried

        rows[:count, edge:] = jnp.zeros_like(rows[:count, edge:])
        if first:
            for tile in range(tiles):
                settle(stations - 1, tile, None)
            lax.fori_loop(1, stations, one, 0)
        else:
            rows[:count, :width] = incoming[...]
            lax.fori_loop(0, stations, one, 0)
        for out in outgoing:
            out[...] = rows[:count, :width]

    @pl.when(lax.axis_index("stn") == turn)
    def _():
        pl.run_scoped(
            run, *[pltpu.ACC(tile % UNITS)((PASS_ROWS, TILE), jnp.float32) for tile in range(tiles)]
        )


def march(turn, block, first, incoming, operator, cosine, sine, forcing, slope, sums):
    held = [pltpu.with_memory_space_constraint(v, pltpu.VMEM) for v in (operator, cosine, sine, forcing, slope)]
    padded = -(-incoming.shape[1] // TILE) * TILE
    results = [jax.ShapeDtypeStruct(sums.shape, sums.dtype)]
    if turn > 0:
        results.append(jax.ShapeDtypeStruct(incoming.shape, incoming.dtype))
    return pl.pallas_call(
        functools.partial(march_kernel, turn, block, first),
        out_shape=results,
        in_specs=[ON_CHIP] * 7,
        out_specs=[ON_CHIP] * len(results),
        scratch_shapes=[pltpu.VMEM((PASS_ROWS, padded), jnp.bfloat16)],
        input_output_aliases={6: 0},
        compiler_params=pltpu.CompilerParams(vmem_limit_bytes=4 << 20),
        name="march",
    )(incoming, *held, sums)


def body(propagator, forcing, forward, damping, slowness, station_gap, freq_index):
    stations, _, width = propagator.shape
    freqs = forcing.shape[2]
    chain = lax.axis_size("stn")
    cosine, sine, slope, edge = prepare(
        station_gap, freq_index, forward, damping[None, :], slowness[None, :]
    )
    half = freqs // BLOCKS
    incoming = [jnp.zeros((2 * half, width), jnp.bfloat16)] * BLOCKS
    sums = jnp.zeros((stations, width), jnp.float32)
    for turn in range(chain):
        here = chain - 1 - turn
        outgoing = []
        for block in range(BLOCKS):
            sums, *out = march(
                here, block, turn == 0, incoming[block],
                propagator, cosine, sine, forcing, slope, sums,
            )
            outgoing += [lax.ppermute(v, "stn", [(here, here - 1)]) for v in out]
        incoming = outgoing
        if turn == 0:
            rim = from_behind(edge, "stn", -1)
            slope = finish(station_gap, rim, slope, sums)
    weighting = 1.0 / (4.0 * math.sqrt(freqs * lax.axis_size("freq")))
    return summed_on_arrival(sums * weighting, "freq", 1)


def solution(mesh):
    placed = (
        P("stn", None, None),
        P("stn", None, "freq", None),
        P("stn", None, "freq", None),
        P(),
        P(),
        P("stn"),
        P("freq"),
    )
    with jax.sharding.use_abstract_mesh(mesh.abstract_mesh):
        return jax.shard_map(
            body, mesh=mesh, in_specs=placed, out_specs=P("stn", "freq"), check_vma=False
        )
```

profile of v0, /device:TPU:0, one launch (start us, length us, event | category | flops | bytes accessed | tf_op | source)
XLA Modules:
  0.0 160.9 jit_solution(7958196573434365854)
XLA Ops:
  0.0 5.9 %prepare.1 = (f32[3,64,2000]{2,1,0:T(8,128)S(1)}, f32[3,64,2000]{2,1,0:T(8,128)S(1)}, f32[3,2,64,2000]{3,2,1,0:T(8,128)S(1)}, bf16[2,64,2000]{2,1,0:T(8,128)(2,1)S(1)}) custom-call(s32[3]{0:T(128)} %gap.1, s32[64]{0:T(128)} %freq_index_hbm.1, bf16[3,2,64,2000]{3,2,1,0:T(8,128)(2,1)} %forward_hbm.1, f32[1,2000]{1,0:T(1,128)} %bitcast.8, f32[1,2000]{1,0:T(1,128)} %bitcast.9), custom_call_target="tpu_custom_call" | custom-call | flops 17179869184 | bytes 67108864 | tf_op jit(solution)/shard_map/prepare/pallas_call | solution.py:101
  5.9 1.6 collective-permute-start.1
  7.6 1.0 slice-done.5
  11.8 0.7 collective-permute-start.3
  12.5 0.7 collective-permute-start.6
  13.3 0.7 collective-permute-start.5
  14.0 0.7 collective-permute-start.8
  14.7 0.7 collective-permute-start.7
  15.4 0.9 collective-permute-start.10
  16.3 0.7 collective-permute-start.9
  17.1 0.7 collective-permute-start.12
  17.8 0.7 collective-permute-start.11
  18.5 0.7 collective-permute-start.14
  19.2 0.7 collective-permute-start.13
  19.9 0.7 collective-permute-start.16
  20.7 0.7 collective-permute-start.15
  21.4 0.7 collective-permute-start.18
  30.3 1.3 collective-permute-start.30
  31.6 1.3 collective-permute-start.29
  32.9 107.0 %collective-permute-done.30.incoming = bf16[64,2000]{1,0:T(8,128)(2,1)S(1)} collective-permute-done((bf16[64,2000]{1,0:T(8,128)(2,1)S(1)}, bf16[64,2000]{1,0:T(8,128)(2,1)S(1)}, u32[]{:S(2)}, u32[]{:S(2)}) %collective-permute-start.30) | collective-permute-done | bytes 256032 | tf_op jit(solution)/shard_map/ppermute | solution.py:289
  139.9 4.1 %march.62.sums_in = f32[3,2000]{1,0:T(4,128)S(1)} custom-call(bf16[64,2000]{1,0:T(8,128)(2,1)S(1)} %collective-permute-done.30.incoming, bf16[3,2000,2000]{2,1,0:T(8,128)(2,1)S(1)} %bitcast.6, f32[3,64,2000]{2,1,0:T(8,128)S(1)} %get-tuple-element.69.cosine, f32[3,64,2000]{2,1,0:T(8,128)S(1)} %get-tuple-element.70.sine, ...), custom_call_target="tpu_custom_call", output_to_operand_aliasing={{}: (6, {})} | custom-call | tf_op jit(solution)/shard_map/march/pallas_call | solution.py:259
  143.9 1.6 collective-permute-done.29.incoming
  145.5 4.1 %march.63 = f32[3,2000]{1,0:T(4,128)S(1)} custom-call(bf16[64,2000]{1,0:T(8,128)(2,1)S(1)} %collective-permute-done.29.incoming, bf16[3,2000,2000]{2,1,0:T(8,128)(2,1)S(1)} %bitcast.6, f32[3,64,2000]{2,1,0:T(8,128)S(1)} %get-tuple-element.69.cosine, f32[3,64,2000]{2,1,0:T(8,128)S(1)} %get-tuple-element.70.sine, ...), custom_call_target="tpu_custom_call", output_to_operand_aliasing={{}: (6, {})} | custom-call | tf_op jit(solution)/shard_map/march/pallas_call | solution.py:259
  149.7 10.6 %all_to_all.5 = f32[8,3,250]{2,1,0:T(4,128)S(1)} all-to-all(f32[8,3,250]{2,1,0:T(4,128)S(1)} %bitcast.7), channel_id=1, replica_groups=mesh['stn'=16,'freq'=8] {'freq'}, dimensions={0} | all-to-all | bytes 48000 | tf_op jit(solution)/shard_map/all_to_all | solution.py:39
  (96 shorter events, 12.1 us)
Async XLA Ops:
  5.9 4.4 %collective-permute-start.1 = (bf16[2,64,2000]{2,1,0:T(8,128)(2,1)S(1)}, bf16[2,64,2000]{2,1,0:T(8,128)(2,1)S(1)}, u32[]{:S(2)}, u32[]{:S(2)}) collective-permute-start(bf16[2,64,2000]{2,1,0:T(8,128)(2,1)S(1)} %get-tuple-element.74), channel_id=1, source_target_pairs={{8,0},{16,8},{24,16},{32,24},{40,32},{48,40},{56,48},{64,56},{72,6... | collective-permute-start | bytes 1536008 | tf_op jit(solution)/shard_map/ppermute | solution.py:28
  9.0 2.1 %collective-permute-start.2 = (bf16[64,2000]{1,0:T(8,128)(2,1)S(1)}, bf16[64,2000]{1,0:T(8,128)(2,1)S(1)}, u32[]{:S(2)}, u32[]{:S(2)}) collective-permute-start(bf16[64,2000]{1,0:T(8,128)(2,1)S(1)} %get-tuple-element.76), channel_id=1, source_target_pairs={{120,112},{121,113},{122,114},{123,115},{124,116},{125,117},{126,1... | collective-permute-start | bytes 768008 | tf_op jit(solution)/shard_map/ppermute | solution.py:289
  9.7 2.1 %collective-permute-start = (bf16[64,2000]{1,0:T(8,128)(2,1)S(1)}, bf16[64,2000]{1,0:T(8,128)(2,1)S(1)}, u32[]{:S(2)}, u32[]{:S(2)}) collective-permute-start(bf16[64,2000]{1,0:T(8,128)(2,1)S(1)} %get-tuple-element.73), channel_id=1, source_target_pairs={{120,112},{121,113},{122,114},{123,115},{124,116},{125,117},{126,1... | collective-permute-start | bytes 768008 | tf_op jit(solution)/shard_map/ppermute | solution.py:289
  11.8 1.4 collective-permute-start.3
  12.5 1.4 collective-permute-start.6
  13.3 1.4 collective-permute-start.5
  14.0 1.4 collective-permute-start.8
  14.7 1.6 collective-permute-start.7
  15.4 1.6 collective-permute-start.10
  16.3 1.4 collective-permute-start.9
  17.1 1.4 collective-permute-start.12
  17.8 1.4 collective-permute-start.11
  18.5 1.4 collective-permute-start.14
  19.2 1.4 collective-permute-start.13
  19.9 1.4 collective-permute-start.16
  20.7 1.4 collective-permute-start.15
  21.4 1.4 collective-permute-start.18
  22.1 1.4 collective-permute-start.17
  22.8 1.4 collective-permute-start.20
  23.5 1.4 collective-permute-start.19
  27.9 1.6 %collective-permute-start.25 = (bf16[64,2000]{1,0:T(8,128)(2,1)S(1)}, bf16[64,2000]{1,0:T(8,128)(2,1)S(1)}, u32[]{:S(2)}, u32[]{:S(2)}) collective-permute-start(bf16[64,2000]{1,0:T(8,128)(2,1)S(1)} %get-tuple-element.122), channel_id=1, source_target_pairs={{24,16},{25,17},{26,18},{27,19},{28,20},{29,21},{30,22},{31,23}} | collective-permute-start | bytes 768008 | tf_op jit(solution)/shard_map/ppermute | solution.py:289
  29.5 2.0 %collective-permute-start.27 = (bf16[64,2000]{1,0:T(8,128)(2,1)S(1)}, bf16[64,2000]{1,0:T(8,128)(2,1)S(1)}, u32[]{:S(2)}, u32[]{:S(2)}) collective-permute-start(bf16[64,2000]{1,0:T(8,128)(2,1)S(1)} %get-tuple-element.126), channel_id=1, source_target_pairs={{16,8},{17,9},{18,10},{19,11},{20,12},{21,13},{22,14},{23,15}} | collective-permute-start | bytes 768008 | tf_op jit(solution)/shard_map/ppermute | solution.py:289
  30.3 109.6 %collective-permute-start.30 = (bf16[64,2000]{1,0:T(8,128)(2,1)S(1)}, bf16[64,2000]{1,0:T(8,128)(2,1)S(1)}, u32[]{:S(2)}, u32[]{:S(2)}) collective-permute-start(bf16[64,2000]{1,0:T(8,128)(2,1)S(1)} %get-tuple-element.131), channel_id=1, source_target_pairs={{8,0},{9,1},{10,2},{11,3},{12,4},{13,5},{14,6},{15,7}} | collective-permute-start | bytes 768008 | tf_op jit(solution)/shard_map/ppermute | solution.py:289
  31.6 113.9 %collective-permute-start.29 = (bf16[64,2000]{1,0:T(8,128)(2,1)S(1)}, bf16[64,2000]{1,0:T(8,128)(2,1)S(1)}, u32[]{:S(2)}, u32[]{:S(2)}) collective-permute-start(bf16[64,2000]{1,0:T(8,128)(2,1)S(1)} %get-tuple-element.130), channel_id=1, source_target_pairs={{8,0},{9,1},{10,2},{11,3},{12,4},{13,5},{14,6},{15,7}} | collective-permute-start | bytes 768008 | tf_op jit(solution)/shard_map/ppermute | solution.py:289
  (15 other events, 66.0 us)
where the time goes:
time: 161 us
  waiting for transfers between devices  109 us (68%)
  starting transfers between devices  23.3 us (14%)
  Pallas kernels  15.5 us (10%)
  blocking collectives  10.6 us (7%)
    ppermute x30, waiting for transfers between devices, body(): outgoing += [lax.ppermute(v, 'stn', [(here, here - 1)]) for v in out]  109 us
    ppermute x30, starting transfers between devices, body(): outgoing += [lax.ppermute(v, 'stn', [(here, here - 1)]) for v in out]  21.7 us
    all_to_all x1, blocking collectives, summed_on_arrival(): lax.all_to_all(in_blocks(value, dim, length), axis, 0, 0, tiled=True)  10.6 us
    pallas_call x32, Pallas kernels, march(): pl.pallas_call(functools.partial(march_kernel, turn, block, first), out_s...  8.89 us
    pallas_call x1, Pallas kernels, prepare(): pl.pallas_call(prepare_kernel, out_shape=(pltpu.VMEM((stations, freqs, wi...  5.9 us
  transfers between devices with their start and end apart: 31, of which 2 were waited for; matrix products, arithmetic and copies ran while one was open for 0% of the time, Pallas kernels for 3%

commit v1 on v0

--- a/solution.py
+++ b/solution.py
@@ -22,10 +22,9 @@
 SCALARS = pl.BlockSpec(memory_space=pltpu.SMEM)
 
 
-def from_behind(value, axis, by):
-    length = lax.axis_size(axis)
-    pairs = [(i, i + by) for i in range(length) if 0 <= i + by < length]
-    return lax.ppermute(value, axis, pairs)
+def from_next(value, parity):
+    pairs = [(i, i - 1) for i in range(1, lax.axis_size("stn")) if i % 2 == parity]
+    return lax.ppermute(value, "stn", pairs)
 
 
 def in_blocks(value, dim, length):
@@ -275,6 +274,7 @@
     cosine, sine, slope, edge = prepare(
         station_gap, freq_index, forward, damping[None, :], slowness[None, :]
     )
+    rim = from_next(edge, 1)
     half = freqs // BLOCKS
     incoming = [jnp.zeros((2 * half, width), jnp.bfloat16)] * BLOCKS
     sums = jnp.zeros((stations, width), jnp.float32)
@@ -289,7 +289,10 @@
             outgoing += [lax.ppermute(v, "stn", [(here, here - 1)]) for v in out]
         incoming = outgoing
         if turn == 0:
-            rim = from_behind(edge, "stn", -1)
+            slope = finish(station_gap, rim, slope, sums)
+            edge, _ = lax.optimization_barrier((edge, sums))
+            rim = from_next(edge, 0)
+        elif turn == 1:
             slope = finish(station_gap, rim, slope, sums)
     weighting = 1.0 / (4.0 * math.sqrt(freqs * lax.axis_size("freq")))
     return summed_on_arrival(sums * weighting, "freq", 1)

time: 161 us -> 159 us (0.988)
  waiting for transfers between devices: 109 us -> 105 us
    ppermute x30, waiting for transfers between devices: 109 us -> 105 us  [body(): outgoing += [lax.ppermute(v, 'stn', [(here, here - 1)]) for v in out]]
  transfers between devices with their start and end apart: 31 -> 32, of which waited for: 2 -> 2; matrix products, arithmetic and copies ran while one was open for 0% -> 0% of each run, Pallas kernels for 3% -> 4%
where the time goes in v1:
time: 159 us
  waiting for transfers between devices  105 us (66%)
  starting transfers between devices  23.8 us (15%)
  Pallas kernels  16.3 us (10%)
  blocking collectives  10.6 us (7%)
    ppermute x30, waiting for transfers between devices, body(): outgoing += [lax.ppermute(v, 'stn', [(here, here - 1)]) for v in out]  105 us
    ppermute x30, starting transfers between devices, body(): outgoing += [lax.ppermute(v, 'stn', [(here, here - 1)]) for v in out]  21.5 us
    all_to_all x1, blocking collectives, summed_on_arrival(): lax.all_to_all(in_blocks(value, dim, length), axis, 0, 0, tiled=True)  10.6 us
    pallas_call x32, Pallas kernels, march(): pl.pallas_call(functools.partial(march_kernel, turn, block, first), out_s...  9.07 us
    pallas_call x1, Pallas kernels, prepare(): pl.pallas_call(prepare_kernel, out_shape=(pltpu.VMEM((stations, freqs, wi...  5.9 us
  transfers between devices with their start and end apart: 32, of which 2 were waited for; matrix products, arithmetic and copies ran while one was open for 0% of the time, Pallas kernels for 4%

profile of v1, /device:TPU:0, one launch (start us, length us, event | category | flops | bytes accessed | tf_op | source)
XLA Modules:
  0.0 159.0 jit_solution(5200691606217465490)
XLA Ops:
  0.0 5.9 %prepare.1 = (f32[3,64,2000]{2,1,0:T(8,128)S(1)}, f32[3,64,2000]{2,1,0:T(8,128)S(1)}, f32[3,2,64,2000]{3,2,1,0:T(8,128)S(1)}, bf16[2,64,2000]{2,1,0:T(8,128)(2,1)S(1)}) custom-call(s32[3]{0:T(128)} %gap.3, s32[64]{0:T(128)} %freq_index_hbm.1, bf16[3,2,64,2000]{3,2,1,0:T(8,128)(2,1)} %forward_hbm.1, f32[1,2000]{1,0:T(1,128)} %bitcast.8, f32[1,2000]{1,0:T(1,128)} %bitcast.9), custom_call_target="tpu_custom_call" | custom-call | flops 17179869184 | bytes 67108864 | tf_op jit(solution)/shard_map/prepare/pallas_call | solution.py:100
  5.9 1.6 collective-permute-start.1
  7.6 1.0 slice-done.5
  9.7 0.7 collective-permute-start.4
  10.4 0.7 collective-permute-start
  11.8 0.7 collective-permute-start.5
  22.8 0.7 collective-permute-start.19
  23.5 0.7 collective-permute-start.18
  24.2 0.7 collective-permute-start.21
  24.9 0.7 collective-permute-start.20
  25.6 0.7 collective-permute-start.23
  26.4 0.7 collective-permute-start.22
  27.1 0.7 collective-permute-start.25
  27.8 0.7 collective-permute-start.24
  29.5 0.7 collective-permute-start.26
  30.2 0.7 collective-permute-start.29
  30.9 0.7 collective-permute-start.28
  31.6 1.3 collective-permute-start.31
  33.0 1.3 collective-permute-start.30
  34.3 103.6 %collective-permute-done.31.incoming = bf16[64,2000]{1,0:T(8,128)(2,1)S(1)} collective-permute-done((bf16[64,2000]{1,0:T(8,128)(2,1)S(1)}, bf16[64,2000]{1,0:T(8,128)(2,1)S(1)}, u32[]{:S(2)}, u32[]{:S(2)}) %collective-permute-start.31) | collective-permute-done | bytes 256032 | tf_op jit(solution)/shard_map/ppermute | solution.py:289
  137.9 4.1 %march.62.sums_in = f32[3,2000]{1,0:T(4,128)S(1)} custom-call(bf16[64,2000]{1,0:T(8,128)(2,1)S(1)} %collective-permute-done.31.incoming, bf16[3,2000,2000]{2,1,0:T(8,128)(2,1)S(1)} %bitcast.6, f32[3,64,2000]{2,1,0:T(8,128)S(1)} %get-tuple-element.70.cosine, f32[3,64,2000]{2,1,0:T(8,128)S(1)} %get-tuple-element.71.sine, ...), custom_call_target="tpu_custom_call", output_to_operand_aliasing={{}: (6, {})} | custom-call | tf_op jit(solution)/shard_map/march/pallas_call | solution.py:258
  142.0 1.6 %collective-permute-done.30.incoming = bf16[64,2000]{1,0:T(8,128)(2,1)S(1)} collective-permute-done((bf16[64,2000]{1,0:T(8,128)(2,1)S(1)}, bf16[64,2000]{1,0:T(8,128)(2,1)S(1)}, u32[]{:S(2)}, u32[]{:S(2)}) %collective-permute-start.30) | collective-permute-done | bytes 256032 | tf_op jit(solution)/shard_map/ppermute | solution.py:289
  143.6 4.1 %march.63 = f32[3,2000]{1,0:T(4,128)S(1)} custom-call(bf16[64,2000]{1,0:T(8,128)(2,1)S(1)} %collective-permute-done.30.incoming, bf16[3,2000,2000]{2,1,0:T(8,128)(2,1)S(1)} %bitcast.6, f32[3,64,2000]{2,1,0:T(8,128)S(1)} %get-tuple-element.70.cosine, f32[3,64,2000]{2,1,0:T(8,128)S(1)} %get-tuple-element.71.sine, ...), custom_call_target="tpu_custom_call", output_to_operand_aliasing={{}: (6, {})} | custom-call | tf_op jit(solution)/shard_map/march/pallas_call | solution.py:258
  147.8 10.6 %all_to_all.5 = f32[8,3,250]{2,1,0:T(4,128)S(1)} all-to-all(f32[8,3,250]{2,1,0:T(4,128)S(1)} %bitcast.7), channel_id=1, replica_groups=mesh['stn'=16,'freq'=8] {'freq'}, dimensions={0} | all-to-all | bytes 48000 | tf_op jit(solution)/shard_map/all_to_all | solution.py:38
  (99 shorter events, 13.7 us)
Async XLA Ops:
  5.9 5.1 %collective-permute-start.1 = (bf16[2,64,2000]{2,1,0:T(8,128)(2,1)S(1)}, bf16[2,64,2000]{2,1,0:T(8,128)(2,1)S(1)}, u32[]{:S(2)}, u32[]{:S(2)}) collective-permute-start(bf16[2,64,2000]{2,1,0:T(8,128)(2,1)S(1)} %get-tuple-element.80), channel_id=1, source_target_pairs={{8,0},{24,16},{40,32},{56,48},{72,64},{88,80},{104,96},{120,112},{... | collective-permute-start | bytes 1536008 | tf_op jit(solution)/shard_map/ppermute | solution.py:27
  9.0 2.8 %collective-permute-start.2 = (bf16[64,2000]{1,0:T(8,128)(2,1)S(1)}, bf16[64,2000]{1,0:T(8,128)(2,1)S(1)}, u32[]{:S(2)}, u32[]{:S(2)}) collective-permute-start(bf16[64,2000]{1,0:T(8,128)(2,1)S(1)} %get-tuple-element.77), channel_id=1, source_target_pairs={{120,112},{121,113},{122,114},{123,115},{124,116},{125,117},{126,1... | collective-permute-start | bytes 768008 | tf_op jit(solution)/shard_map/ppermute | solution.py:289
  9.7 3.5 %collective-permute-start.4 = (bf16[2,64,2000]{2,1,0:T(8,128)(2,1)S(1)}, bf16[2,64,2000]{2,1,0:T(8,128)(2,1)S(1)}, u32[]{:S(2)}, u32[]{:S(2)}) collective-permute-start(bf16[2,64,2000]{2,1,0:T(8,128)(2,1)S(1)} %get-tuple-element.80), channel_id=1, source_target_pairs={{16,8},{32,24},{48,40},{64,56},{80,72},{96,88},{112,104},{17,9},{3... | collective-permute-start | bytes 1536008 | tf_op jit(solution)/shard_map/ppermute | solution.py:27
  10.4 2.1 %collective-permute-start = (bf16[64,2000]{1,0:T(8,128)(2,1)S(1)}, bf16[64,2000]{1,0:T(8,128)(2,1)S(1)}, u32[]{:S(2)}, u32[]{:S(2)}) collective-permute-start(bf16[64,2000]{1,0:T(8,128)(2,1)S(1)} %get-tuple-element.74), channel_id=1, source_target_pairs={{120,112},{121,113},{122,114},{123,115},{124,116},{125,117},{126,1... | collective-permute-start | bytes 768008 | tf_op jit(solution)/shard_map/ppermute | solution.py:289
  11.8 2.1 %collective-permute-start.5 = (bf16[64,2000]{1,0:T(8,128)(2,1)S(1)}, bf16[64,2000]{1,0:T(8,128)(2,1)S(1)}, u32[]{:S(2)}, u32[]{:S(2)}) collective-permute-start(bf16[64,2000]{1,0:T(8,128)(2,1)S(1)} %get-tuple-element.82), channel_id=1, source_target_pairs={{112,104},{113,105},{114,106},{115,107},{116,108},{117,109},{118,1... | collective-permute-start | bytes 768008 | tf_op jit(solution)/shard_map/ppermute | solution.py:289
  12.5 2.1 %collective-permute-start.3 = (bf16[64,2000]{1,0:T(8,128)(2,1)S(1)}, bf16[64,2000]{1,0:T(8,128)(2,1)S(1)}, u32[]{:S(2)}, u32[]{:S(2)}) collective-permute-start(bf16[64,2000]{1,0:T(8,128)(2,1)S(1)} %get-tuple-element.79), channel_id=1, source_target_pairs={{112,104},{113,105},{114,106},{115,107},{116,108},{117,109},{118,1... | collective-permute-start | bytes 768008 | tf_op jit(solution)/shard_map/ppermute | solution.py:289
  13.9 1.4 collective-permute-start.7
  16.1 1.6 collective-permute-start.8
  17.0 1.4 collective-permute-start.11
  17.7 1.4 collective-permute-start.10
  22.8 1.4 collective-permute-start.19
  23.5 1.4 collective-permute-start.18
  24.2 1.4 collective-permute-start.21
  24.9 1.4 collective-permute-start.20
  25.6 1.4 collective-permute-start.23
  26.4 1.4 collective-permute-start.22
  27.1 1.4 collective-permute-start.25
  27.8 1.4 collective-permute-start.24
  28.5 1.6 %collective-permute-start.27 = (bf16[64,2000]{1,0:T(8,128)(2,1)S(1)}, bf16[64,2000]{1,0:T(8,128)(2,1)S(1)}, u32[]{:S(2)}, u32[]{:S(2)}) collective-permute-start(bf16[64,2000]{1,0:T(8,128)(2,1)S(1)} %get-tuple-element.125), channel_id=1, source_target_pairs={{24,16},{25,17},{26,18},{27,19},{28,20},{29,21},{30,22},{31,23}} | collective-permute-start | bytes 768008 | tf_op jit(solution)/shard_map/ppermute | solution.py:289
  29.5 1.4 collective-permute-start.26
  30.2 1.4 collective-permute-start.29
  30.9 2.0 %collective-permute-start.28 = (bf16[64,2000]{1,0:T(8,128)(2,1)S(1)}, bf16[64,2000]{1,0:T(8,128)(2,1)S(1)}, u32[]{:S(2)}, u32[]{:S(2)}) collective-permute-start(bf16[64,2000]{1,0:T(8,128)(2,1)S(1)} %get-tuple-element.128), channel_id=1, source_target_pairs={{16,8},{17,9},{18,10},{19,11},{20,12},{21,13},{22,14},{23,15}} | collective-permute-start | bytes 768008 | tf_op jit(solution)/shard_map/ppermute | solution.py:289
  31.6 106.3 %collective-permute-start.31 = (bf16[64,2000]{1,0:T(8,128)(2,1)S(1)}, bf16[64,2000]{1,0:T(8,128)(2,1)S(1)}, u32[]{:S(2)}, u32[]{:S(2)}) collective-permute-start(bf16[64,2000]{1,0:T(8,128)(2,1)S(1)} %get-tuple-element.133), channel_id=1, source_target_pairs={{8,0},{9,1},{10,2},{11,3},{12,4},{13,5},{14,6},{15,7}} | collective-permute-start | bytes 768008 | tf_op jit(solution)/shard_map/ppermute | solution.py:289
  33.0 110.6 %collective-permute-start.30 = (bf16[64,2000]{1,0:T(8,128)(2,1)S(1)}, bf16[64,2000]{1,0:T(8,128)(2,1)S(1)}, u32[]{:S(2)}, u32[]{:S(2)}) collective-permute-start(bf16[64,2000]{1,0:T(8,128)(2,1)S(1)} %get-tuple-element.132), channel_id=1, source_target_pairs={{8,0},{9,1},{10,2},{11,3},{12,4},{13,5},{14,6},{15,7}} | collective-permute-start | bytes 768008 | tf_op jit(solution)/shard_map/ppermute | solution.py:289
  (16 other events, 68.1 us)

commit v2 on v1

--- a/solution.py
+++ b/solution.py
@@ -40,9 +40,9 @@
 
 
 def prepare_kernel(
-    gap_hbm, freq_index_hbm, forward_hbm, damping_hbm, slowness_hbm,
-    cosine, sine, slope, edge,
-    angle, wide, gap, freq_index, forward, damping, slowness, arrived,
+    gap_hbm, freq_index_hbm, forward_hbm, damping_hbm, slowness_hbm, forcing_hbm,
+    cosine, sine, slope, edge, forcing,
+    angle, wide, gap, freq_index, forward, damping, slowness, forcing_here, powers, arrived,
 ):
     stations, _, freqs, width = forward.shape
     padded = wide.shape[1]
@@ -50,7 +50,7 @@
         pltpu.make_async_copy(source, target, arrived.at[i])
         for i, (source, target) in enumerate((
             (freq_index_hbm, freq_index), (slowness_hbm, slowness), (damping_hbm, damping),
-            (gap_hbm, gap), (forward_hbm, forward),
+            (gap_hbm, gap), (forward_hbm, forward), (forcing_hbm, forcing_here),
         ))
     ]
     for fetch in fetches:
@@ -71,16 +71,22 @@
     has_last = place != 0
     fetches[4].wait()
     edge[...] = forward[0]
+    c2 = c1 * c1 - s1 * s1
+    s2 = 2.0 * (c1 * s1)
+    powers[0, 0] = c1
+    powers[0, 1] = s1
+    powers[1, 0] = c2
+    powers[1, 1] = s2
+    powers[2, 0] = c2 * c1 - s2 * s1
+    powers[2, 1] = c2 * s1 + s2 * c1
+    fetches[5].wait()
     for station in range(stations):
         gap_here = gap[station]
-        c2 = c1 * c1 - s1 * s1
-        s2 = 2.0 * (c1 * s1)
-        c3 = c2 * c1 - s2 * s1
-        s3 = c2 * s1 + s2 * c1
-        cosine[station] = jnp.where(gap_here == 1, c1, jnp.where(gap_here == 2, c2, c3))
-        sine[station] = jnp.where(gap_here == 1, s1, jnp.where(gap_here == 2, s2, s3))
-        spacing = gap_here.astype(jnp.float32)
+        cosine[station] = powers[gap_here - 1, 0]
+        sine[station] = powers[gap_here - 1, 1]
+        per_gap = 1.0 / gap_here.astype(jnp.float32)
         for part in range(2):
+            forcing[station, part] = forcing_here[station, part].astype(jnp.float32)
             here = forward[station, part].astype(jnp.float32)
             wide[:, :width] = here
             profile = wide[...]
@@ -89,12 +95,12 @@
             normal = (0.5 * (up - down))[:, :width]
             if station + 1 < stations:
                 after = forward[station + 1, part].astype(jnp.float32)
-                slope[station, part] = (after - here) / spacing + normal
+                slope[station, part] = (after - here) * per_gap + normal
             else:
-                slope[station, part] = normal - here / spacing
-
-
-def prepare(gap, freq_index, forward, damping, slowness):
+                slope[station, part] = normal - here * per_gap
+
+
+def prepare(gap, freq_index, forward, damping, slowness, forcing):
     stations, parts, freqs, width = forward.shape
     padded = -(-width // LANES) * LANES
     return pl.pallas_call(
@@ -104,9 +110,10 @@
             pltpu.VMEM((stations, freqs, width), jnp.float32),
             pltpu.VMEM((stations, parts, freqs, width), jnp.float32),
             jax.ShapeDtypeStruct((parts, freqs, width), forward.dtype),
+            pltpu.VMEM((stations, parts, freqs, width), jnp.float32),
         ),
-        in_specs=[IN_PLACE] * 5,
-        out_specs=(ON_CHIP,) * 4,
+        in_specs=[IN_PLACE] * 6,
+        out_specs=(ON_CHIP,) * 5,
         scratch_shapes=[
             pltpu.VMEM((freqs, width), jnp.float32),
             pltpu.VMEM((freqs, padded), jnp.float32),
@@ -115,20 +122,22 @@
             pltpu.VMEM(forward.shape, forward.dtype),
             pltpu.VMEM(damping.shape, damping.dtype),
             pltpu.VMEM(slowness.shape, slowness.dtype),
-            pltpu.SemaphoreType.DMA((5,)),
+            pltpu.VMEM(forcing.shape, forcing.dtype),
+            pltpu.VMEM((3, 2, freqs, width), jnp.float32),
+            pltpu.SemaphoreType.DMA((6,)),
         ],
         cost_estimate=pl.CostEstimate(flops=16 << 30, bytes_accessed=64 << 20, transcendentals=0),
-        compiler_params=pltpu.CompilerParams(vmem_limit_bytes=10 << 20),
+        compiler_params=pltpu.CompilerParams(vmem_limit_bytes=14 << 20),
         name="prepare",
-    )(*[pltpu.with_memory_space_constraint(v, pltpu.HBM) for v in (gap, freq_index, forward, damping, slowness)])
+    )(*[pltpu.with_memory_space_constraint(v, pltpu.HBM) for v in (gap, freq_index, forward, damping, slowness, forcing)])
 
 
 def finish_kernel(gap, rim, slope_in, after, slope):
     del slope_in, after
     stations, parts, _, _ = slope.shape
-    spacing = gap[stations - 1].astype(jnp.float32)
+    per_gap = 1.0 / gap[stations - 1].astype(jnp.float32)
     for part in range(parts):
-        slope[stations - 1, part] += rim[part].astype(jnp.float32) / spacing
+        slope[stations - 1, part] += rim[part].astype(jnp.float32) * per_gap
 
 
 def finish(gap, rim, slope, after):
@@ -161,16 +170,17 @@
         start = tile * TILE
         size = min(TILE, width - start)
         cut = slice(start, start + size)
-        real_part = forcing[station, 0, low : low + half, cut].astype(jnp.float32)
-        imag_part = forcing[station, 1, low : low + half, cut].astype(jnp.float32)
+        real_part = forcing[station, 0, low : low + half, cut]
+        imag_part = forcing[station, 1, low : low + half, cut]
         if mixed is not None:
             mixed_re, mixed_im = mixed[:half, :size], mixed[half:count, :size]
             c = cosine[station, low : low + half, cut]
             s = sine[station, low : low + half, cut]
             real_part = c * mixed_re + s * mixed_im + real_part
             imag_part = c * mixed_im - s * mixed_re + imag_part
-        rows[:half, cut] = real_part.astype(jnp.bfloat16)
-        rows[half:count, cut] = imag_part.astype(jnp.bfloat16)
+        for place in (rows, *outgoing):
+            place[:half, cut] = real_part.astype(jnp.bfloat16)
+            place[half:count, cut] = imag_part.astype(jnp.bfloat16)
         product = (
             real_part * slope[station, 0, low : low + half, cut]
             + imag_part * slope[station, 1, low : low + half, cut]
@@ -239,8 +249,6 @@
         else:
             rows[:count, :width] = incoming[...]
             lax.fori_loop(0, stations, one, 0)
-        for out in outgoing:
-            out[...] = rows[:count, :width]
 
     @pl.when(lax.axis_index("stn") == turn)
     def _():
@@ -271,8 +279,8 @@
     stations, _, width = propagator.shape
     freqs = forcing.shape[2]
     chain = lax.axis_size("stn")
-    cosine, sine, slope, edge = prepare(
-        station_gap, freq_index, forward, damping[None, :], slowness[None, :]
+    cosine, sine, slope, edge, forcing = prepare(
+        station_gap, freq_index, forward, damping[None, :], slowness[None, :], forcing
     )
     rim = from_next(edge, 1)
     half = freqs // BLOCKS

time: 159 us -> 159 us (level)
  no operation moved by 1% of the time
where the time goes in v2:
time: 159 us; the launch traced here: 158 us
  waiting for transfers between devices  104 us (65%)
  starting transfers between devices  23.8 us (15%)
  Pallas kernels  16.3 us (10%)
  blocking collectives  10.6 us (7%)
  local copies, waits for them, and re-layouts  1.72 us (1%)
    ppermute x30, waiting for transfers between devices, body(): outgoing += [lax.ppermute(v, 'stn', [(here, here - 1)]) for v in out]  104 us
    ppermute x30, starting transfers between devices, body(): outgoing += [lax.ppermute(v, 'stn', [(here, here - 1)]) for v in out]  21.5 us
    all_to_all x1, blocking collectives, summed_on_arrival(): lax.all_to_all(in_blocks(value, dim, length), axis, 0, 0, tiled=True)  10.6 us
    pallas_call x32, Pallas kernels, march(): pl.pallas_call(functools.partial(march_kernel, turn, block, first), out_s...  8.94 us
    pallas_call x1, Pallas kernels, prepare(): pl.pallas_call(prepare_kernel, out_shape=(pltpu.VMEM((stations, freqs, wi...  5.81 us
  transfers between devices with their start and end apart: 32, of which 2 were waited for; matrix products, arithmetic and copies ran while one was open for 0% of the time, Pallas kernels for 4%

profile of v2, /device:TPU:0, one launch (start us, length us, event | category | flops | bytes accessed | tf_op | source)
XLA Modules:
  0.0 158.3 jit_solution(2881712806560161951)
XLA Ops:
  0.0 5.8 %prepare.1 = (f32[3,64,2000]{2,1,0:T(8,128)S(1)}, f32[3,64,2000]{2,1,0:T(8,128)S(1)}, f32[3,2,64,2000]{3,2,1,0:T(8,128)S(1)}, bf16[2,64,2000]{2,1,0:T(8,128)(2,1)S(1)}, f32[3,2,64,2000]{3,2,1,0:T(8,128)S(1)}) custom-call(s32[3]{0:T(128)} %gap.3, s32[64]{0:T(128)} %freq_index_hbm.1, bf16[3,2,64,2000]{3,2,1,0:T(8,128)(2,1)} %forward_hbm.1, f32[1,2000]{1,0:T(1,128)} %bitcast.8, ...), custom_call_target="tpu_custom_call" | custom-call | flops 17179869184 | bytes 67108864 | tf_op jit(solution)/shard_map/prepare/pallas_call | solution.py:106
  5.8 1.6 collective-permute-start.1
  8.0 1.0 slice-done.5
  9.8 0.7 collective-permute-start.4
  10.5 0.7 collective-permute-start
  11.2 0.8 finish.2.slope.slope_in
  13.4 0.8 finish.3.slope
  14.2 0.7 collective-permute-start.7
  14.9 0.7 collective-permute-start.6
  15.6 0.7 collective-permute-start.9
  16.4 0.7 collective-permute-start.8
  17.3 0.7 collective-permute-start.11
  18.0 0.7 collective-permute-start.10
  18.7 0.7 collective-permute-start.13
  19.4 0.7 collective-permute-start.12
  20.2 0.7 collective-permute-start.15
  20.9 0.7 collective-permute-start.14
  31.9 1.3 collective-permute-start.31
  33.3 1.3 collective-permute-start.30
  34.6 102.8 %collective-permute-done.31.incoming = bf16[64,2000]{1,0:T(8,128)(2,1)S(1)} collective-permute-done((bf16[64,2000]{1,0:T(8,128)(2,1)S(1)}, bf16[64,2000]{1,0:T(8,128)(2,1)S(1)}, u32[]{:S(2)}, u32[]{:S(2)}) %collective-permute-start.31) | collective-permute-done | bytes 256032 | tf_op jit(solution)/shard_map/ppermute | solution.py:297
  137.4 4.0 %march.62.sums_in = f32[3,2000]{1,0:T(4,128)S(1)} custom-call(bf16[64,2000]{1,0:T(8,128)(2,1)S(1)} %collective-permute-done.31.incoming, bf16[3,2000,2000]{2,1,0:T(8,128)(2,1)S(1)} %bitcast.6, f32[3,64,2000]{2,1,0:T(8,128)S(1)} %get-tuple-element.71.cosine, f32[3,64,2000]{2,1,0:T(8,128)S(1)} %get-tuple-element.72.sine, ...), custom_call_target="tpu_custom_call", output_to_operand_aliasing={{}: (6, {})} | custom-call | tf_op jit(solution)/shard_map/march/pallas_call | solution.py:266
  141.4 1.6 %collective-permute-done.30.incoming = bf16[64,2000]{1,0:T(8,128)(2,1)S(1)} collective-permute-done((bf16[64,2000]{1,0:T(8,128)(2,1)S(1)}, bf16[64,2000]{1,0:T(8,128)(2,1)S(1)}, u32[]{:S(2)}, u32[]{:S(2)}) %collective-permute-start.30) | collective-permute-done | bytes 256032 | tf_op jit(solution)/shard_map/ppermute | solution.py:297
  143.0 4.0 %march.63 = f32[3,2000]{1,0:T(4,128)S(1)} custom-call(bf16[64,2000]{1,0:T(8,128)(2,1)S(1)} %collective-permute-done.30.incoming, bf16[3,2000,2000]{2,1,0:T(8,128)(2,1)S(1)} %bitcast.6, f32[3,64,2000]{2,1,0:T(8,128)S(1)} %get-tuple-element.71.cosine, f32[3,64,2000]{2,1,0:T(8,128)S(1)} %get-tuple-element.72.sine, ...), custom_call_target="tpu_custom_call", output_to_operand_aliasing={{}: (6, {})} | custom-call | tf_op jit(solution)/shard_map/march/pallas_call | solution.py:266
  147.1 10.6 %all_to_all.5 = f32[8,3,250]{2,1,0:T(4,128)S(1)} all-to-all(f32[8,3,250]{2,1,0:T(4,128)S(1)} %bitcast.7), channel_id=1, replica_groups=mesh['stn'=16,'freq'=8] {'freq'}, dimensions={0} | all-to-all | bytes 48000 | tf_op jit(solution)/shard_map/all_to_all | solution.py:38
  (97 shorter events, 13.8 us)
Async XLA Ops:
  5.8 5.3 %collective-permute-start.1 = (bf16[2,64,2000]{2,1,0:T(8,128)(2,1)S(1)}, bf16[2,64,2000]{2,1,0:T(8,128)(2,1)S(1)}, u32[]{:S(2)}, u32[]{:S(2)}) collective-permute-start(bf16[2,64,2000]{2,1,0:T(8,128)(2,1)S(1)} %get-tuple-element.82), channel_id=1, source_target_pairs={{8,0},{24,16},{40,32},{56,48},{72,64},{88,80},{104,96},{120,112},{... | collective-permute-start | bytes 1536008 | tf_op jit(solution)/shard_map/ppermute | solution.py:27
  9.1 2.9 %collective-permute-start.2 = (bf16[64,2000]{1,0:T(8,128)(2,1)S(1)}, bf16[64,2000]{1,0:T(8,128)(2,1)S(1)}, u32[]{:S(2)}, u32[]{:S(2)}) collective-permute-start(bf16[64,2000]{1,0:T(8,128)(2,1)S(1)} %get-tuple-element.79), channel_id=1, source_target_pairs={{120,112},{121,113},{122,114},{123,115},{124,116},{125,117},{126,1... | collective-permute-start | bytes 768008 | tf_op jit(solution)/shard_map/ppermute | solution.py:297
  9.8 3.6 %collective-permute-start.4 = (bf16[2,64,2000]{2,1,0:T(8,128)(2,1)S(1)}, bf16[2,64,2000]{2,1,0:T(8,128)(2,1)S(1)}, u32[]{:S(2)}, u32[]{:S(2)}) collective-permute-start(bf16[2,64,2000]{2,1,0:T(8,128)(2,1)S(1)} %get-tuple-element.82), channel_id=1, source_target_pairs={{16,8},{32,24},{48,40},{64,56},{80,72},{96,88},{112,104},{17,9},{3... | collective-permute-start | bytes 1536008 | tf_op jit(solution)/shard_map/ppermute | solution.py:27
  10.5 2.2 %collective-permute-start = (bf16[64,2000]{1,0:T(8,128)(2,1)S(1)}, bf16[64,2000]{1,0:T(8,128)(2,1)S(1)}, u32[]{:S(2)}, u32[]{:S(2)}) collective-permute-start(bf16[64,2000]{1,0:T(8,128)(2,1)S(1)} %get-tuple-element.76), channel_id=1, source_target_pairs={{120,112},{121,113},{122,114},{123,115},{124,116},{125,117},{126,1... | collective-permute-start | bytes 768008 | tf_op jit(solution)/shard_map/ppermute | solution.py:297
  12.0 2.2 %collective-permute-start.5 = (bf16[64,2000]{1,0:T(8,128)(2,1)S(1)}, bf16[64,2000]{1,0:T(8,128)(2,1)S(1)}, u32[]{:S(2)}, u32[]{:S(2)}) collective-permute-start(bf16[64,2000]{1,0:T(8,128)(2,1)S(1)} %get-tuple-element.84), channel_id=1, source_target_pairs={{112,104},{113,105},{114,106},{115,107},{116,108},{117,109},{118,1... | collective-permute-start | bytes 768008 | tf_op jit(solution)/shard_map/ppermute | solution.py:297
  12.7 2.2 %collective-permute-start.3 = (bf16[64,2000]{1,0:T(8,128)(2,1)S(1)}, bf16[64,2000]{1,0:T(8,128)(2,1)S(1)}, u32[]{:S(2)}, u32[]{:S(2)}) collective-permute-start(bf16[64,2000]{1,0:T(8,128)(2,1)S(1)} %get-tuple-element.81), channel_id=1, source_target_pairs={{112,104},{113,105},{114,106},{115,107},{116,108},{117,109},{118,1... | collective-permute-start | bytes 768008 | tf_op jit(solution)/shard_map/ppermute | solution.py:297
  14.2 1.4 collective-permute-start.7
  14.9 1.4 collective-permute-start.6
  15.6 1.4 collective-permute-start.9
  16.4 1.6 %collective-permute-start.8 = (bf16[64,2000]{1,0:T(8,128)(2,1)S(1)}, bf16[64,2000]{1,0:T(8,128)(2,1)S(1)}, u32[]{:S(2)}, u32[]{:S(2)}) collective-permute-start(bf16[64,2000]{1,0:T(8,128)(2,1)S(1)} %get-tuple-element.90), channel_id=1, source_target_pairs={{96,88},{97,89},{98,90},{99,91},{100,92},{101,93},{102,94},{103,95}} | collective-permute-start | bytes 768008 | tf_op jit(solution)/shard_map/ppermute | solution.py:297
  17.3 1.4 collective-permute-start.11
  18.0 1.4 collective-permute-start.10
  18.7 1.4 collective-permute-start.13
  19.4 1.4 collective-permute-start.12
  20.2 1.4 collective-permute-start.15
  20.9 1.4 collective-permute-start.14
  21.6 1.4 collective-permute-start.17
  22.3 1.4 collective-permute-start.16
  23.0 1.4 collective-permute-start.19
  23.8 1.4 collective-permute-start.18
  28.8 1.6 %collective-permute-start.27 = (bf16[64,2000]{1,0:T(8,128)(2,1)S(1)}, bf16[64,2000]{1,0:T(8,128)(2,1)S(1)}, u32[]{:S(2)}, u32[]{:S(2)}) collective-permute-start(bf16[64,2000]{1,0:T(8,128)(2,1)S(1)} %get-tuple-element.127), channel_id=1, source_target_pairs={{24,16},{25,17},{26,18},{27,19},{28,20},{29,21},{30,22},{31,23}} | collective-permute-start | bytes 768008 | tf_op jit(solution)/shard_map/ppermute | solution.py:297
  31.2 2.0 %collective-permute-start.28 = (bf16[64,2000]{1,0:T(8,128)(2,1)S(1)}, bf16[64,2000]{1,0:T(8,128)(2,1)S(1)}, u32[]{:S(2)}, u32[]{:S(2)}) collective-permute-start(bf16[64,2000]{1,0:T(8,128)(2,1)S(1)} %get-tuple-element.130), channel_id=1, source_target_pairs={{16,8},{17,9},{18,10},{19,11},{20,12},{21,13},{22,14},{23,15}} | collective-permute-start | bytes 768008 | tf_op jit(solution)/shard_map/ppermute | solution.py:297
  31.9 105.4 %collective-permute-start.31 = (bf16[64,2000]{1,0:T(8,128)(2,1)S(1)}, bf16[64,2000]{1,0:T(8,128)(2,1)S(1)}, u32[]{:S(2)}, u32[]{:S(2)}) collective-permute-start(bf16[64,2000]{1,0:T(8,128)(2,1)S(1)} %get-tuple-element.135), channel_id=1, source_target_pairs={{8,0},{9,1},{10,2},{11,3},{12,4},{13,5},{14,6},{15,7}} | collective-permute-start | bytes 768008 | tf_op jit(solution)/shard_map/ppermute | solution.py:297
  33.3 109.7 %collective-permute-start.30 = (bf16[64,2000]{1,0:T(8,128)(2,1)S(1)}, bf16[64,2000]{1,0:T(8,128)(2,1)S(1)}, u32[]{:S(2)}, u32[]{:S(2)}) collective-permute-start(bf16[64,2000]{1,0:T(8,128)(2,1)S(1)} %get-tuple-element.134), channel_id=1, source_target_pairs={{8,0},{9,1},{10,2},{11,3},{12,4},{13,5},{14,6},{15,7}} | collective-permute-start | bytes 768008 | tf_op jit(solution)/shard_map/ppermute | solution.py:297
  (15 other events, 59.6 us)

commit v3 on v2

--- a/solution.py
+++ b/solution.py
@@ -155,16 +155,17 @@
 def march_kernel(
     turn, block, first, incoming, operator, cosine, sine, forcing, slope, sums_in, *results,
 ):
-    sums, outgoing, rows = results[0], results[1:-1], results[-1]
+    sums, rows = results
+    repeat = PASS_ROWS // incoming.shape[0]
     stations, freqs, width = cosine.shape
-    half = incoming.shape[0] // 2
+    half = rows.shape[0] // 2
     count = 2 * half
     low = block * half
     full = width // TILE
     rest = width - full * TILE
     tiles = full + 1
     groups = tiles // UNITS
-    edge = width // LANES * LANES
+    del incoming
 
     def settle(station, tile, mixed):
         start = tile * TILE
@@ -178,9 +179,8 @@
             s = sine[station, low : low + half, cut]
             real_part = c * mixed_re + s * mixed_im + real_part
             imag_part = c * mixed_im - s * mixed_re + imag_part
-        for place in (rows, *outgoing):
-            place[:half, cut] = real_part.astype(jnp.bfloat16)
-            place[half:count, cut] = imag_part.astype(jnp.bfloat16)
+        rows[:half, cut] = real_part.astype(jnp.bfloat16)
+        rows[half:, cut] = imag_part.astype(jnp.bfloat16)
         product = (
             real_part * slope[station, 0, low : low + half, cut]
             + imag_part * slope[station, 1, low : low + half, cut]
@@ -213,7 +213,8 @@
                     pltpu.matmul_push_rhs(piece(depth, UNITS * group + unit), group % 2, unit)
 
             def state_at(depth):
-                return rows[:, pl.ds(pl.multiple_of(depth * TILE, TILE), TILE)]
+                held = rows[:, pl.ds(pl.multiple_of(depth * TILE, TILE), TILE)]
+                return jnp.concatenate([held] * repeat, axis=0)
 
             def accumulate(state, group):
                 for unit in range(UNITS):
@@ -232,7 +233,7 @@
             push(0, 0)
             lax.fori_loop(0, full - 1, deepen, 0)
             deepen(full - 1, 0)
-            state = rows[:, full * TILE :]
+            state = state_at(full)
             for group in range(groups):
                 if group + 1 < groups:
                     push(full, group + 1)
@@ -241,13 +242,11 @@
                 settle(station, tile, pltpu.matmul_pop(sums_of[tile]))
             return carried
 
-        rows[:count, edge:] = jnp.zeros_like(rows[:count, edge:])
         if first:
             for tile in range(tiles):
                 settle(stations - 1, tile, None)
             lax.fori_loop(1, stations, one, 0)
         else:
-            rows[:count, :width] = incoming[...]
             lax.fori_loop(0, stations, one, 0)
 
     @pl.when(lax.axis_index("stn") == turn)
@@ -259,20 +258,15 @@
 
 def march(turn, block, first, incoming, operator, cosine, sine, forcing, slope, sums):
     held = [pltpu.with_memory_space_constraint(v, pltpu.VMEM) for v in (operator, cosine, sine, forcing, slope)]
-    padded = -(-incoming.shape[1] // TILE) * TILE
-    results = [jax.ShapeDtypeStruct(sums.shape, sums.dtype)]
-    if turn > 0:
-        results.append(jax.ShapeDtypeStruct(incoming.shape, incoming.dtype))
     return pl.pallas_call(
         functools.partial(march_kernel, turn, block, first),
-        out_shape=results,
+        out_shape=[jax.ShapeDtypeStruct(v.shape, v.dtype) for v in (sums, incoming)],
         in_specs=[ON_CHIP] * 7,
-        out_specs=[ON_CHIP] * len(results),
-        scratch_shapes=[pltpu.VMEM((PASS_ROWS, padded), jnp.bfloat16)],
-        input_output_aliases={6: 0},
+        out_specs=[ON_CHIP] * 2,
+        input_output_aliases={6: 0, 0: 1},
         compiler_params=pltpu.CompilerParams(vmem_limit_bytes=4 << 20),
         name="march",
-    )(incoming, *held, sums)
+    )(pltpu.with_memory_space_constraint(incoming, pltpu.VMEM), *held, sums)
 
 
 def body(propagator, forcing, forward, damping, slowness, station_gap, freq_index):
@@ -284,17 +278,19 @@
     )
     rim = from_next(edge, 1)
     half = freqs // BLOCKS
-    incoming = [jnp.zeros((2 * half, width), jnp.bfloat16)] * BLOCKS
+    padded = -(-width // TILE) * TILE
+    incoming = [jnp.zeros((2 * half, padded), jnp.bfloat16)] * BLOCKS
     sums = jnp.zeros((stations, width), jnp.float32)
     for turn in range(chain):
         here = chain - 1 - turn
         outgoing = []
         for block in range(BLOCKS):
-            sums, *out = march(
+            sums, out = march(
                 here, block, turn == 0, incoming[block],
                 propagator, cosine, sine, forcing, slope, sums,
             )
-            outgoing += [lax.ppermute(v, "stn", [(here, here - 1)]) for v in out]
+            if here > 0:
+                outgoing.append(lax.ppermute(out, "stn", [(here, here - 1)]))
         incoming = outgoing
         if turn == 0:
             slope = finish(station_gap, rim, slope, sums)

time: 159 us -> 157 us (0.987)
  no operation moved by 1% of the time
where the time goes in v3:
time: 157 us
  waiting for transfers between devices  103 us (66%)
  starting transfers between devices  23.8 us (15%)
  Pallas kernels  16.1 us (10%)
  blocking collectives  10.6 us (7%)
  local copies, waits for them, and re-layouts  1.74 us (1%)
    ppermute x30, waiting for transfers between devices, body(): outgoing.append(lax.ppermute(out, 'stn', [(here, here - 1)]))  103 us
    ppermute x30, starting transfers between devices, body(): outgoing.append(lax.ppermute(out, 'stn', [(here, here - 1)]))  21.5 us
    all_to_all x1, blocking collectives, summed_on_arrival(): lax.all_to_all(in_blocks(value, dim, length), axis, 0, 0, tiled=True)  10.6 us
    pallas_call x32, Pallas kernels, march(): pl.pallas_call(functools.partial(march_kernel, turn, block, first), out_s...  8.76 us
    pallas_call x1, Pallas kernels, prepare(): pl.pallas_call(prepare_kernel, out_shape=(pltpu.VMEM((stations, freqs, wi...  5.81 us
  transfers between devices with their start and end apart: 32, of which 2 were waited for; matrix products, arithmetic and copies ran while one was open for 0% of the time, Pallas kernels for 4%

profile of v3, /device:TPU:0, one launch (start us, length us, event | category | flops | bytes accessed | tf_op | source)
XLA Modules:
  0.0 156.6 jit_solution(14176834909834435653)
XLA Ops:
  0.0 5.8 %prepare.1 = (f32[3,64,2000]{2,1,0:T(8,128)S(1)}, f32[3,64,2000]{2,1,0:T(8,128)S(1)}, f32[3,2,64,2000]{3,2,1,0:T(8,128)S(1)}, bf16[2,64,2000]{2,1,0:T(8,128)(2,1)S(1)}, f32[3,2,64,2000]{3,2,1,0:T(8,128)S(1)}) custom-call(s32[3]{0:T(128)} %gap.3, s32[64]{0:T(128)} %freq_index_hbm.1, bf16[3,2,64,2000]{3,2,1,0:T(8,128)(2,1)} %forward_hbm.1, f32[1,2000]{1,0:T(1,128)} %bitcast.8, ...), custom_call_target="tpu_custom_call" | custom-call | flops 17179869184 | bytes 67108864 | tf_op jit(solution)/shard_map/prepare/pallas_call | solution.py:106
  5.8 1.6 collective-permute-start.1
  8.0 1.0 slice-done.5
  9.8 0.7 collective-permute-start
  10.5 0.7 collective-permute-start.4
  11.2 0.8 finish.2.slope.slope_in
  12.7 0.7 collective-permute-start.3
  13.4 0.8 finish.3.slope
  15.0 0.7 collective-permute-start.6
  17.1 0.7 collective-permute-start.11
  19.5 0.7 collective-permute-start.12
  20.2 0.7 collective-permute-start.15
  22.4 0.7 collective-permute-start.16
  25.2 0.7 collective-permute-start.20
  27.4 0.7 collective-permute-start.25
  28.1 0.7 collective-permute-start.24
  30.3 0.7 collective-permute-start.29
  32.0 1.3 collective-permute-start.31
  33.3 1.3 collective-permute-start.30
  34.6 101.2 %collective-permute-done.31.incoming = bf16[64,2048]{1,0:T(8,128)(2,1)S(1)} collective-permute-done((bf16[64,2048]{1,0:T(8,128)(2,1)S(1)}, bf16[64,2048]{1,0:T(8,128)(2,1)S(1)}, u32[]{:S(2)}, u32[]{:S(2)}) %collective-permute-start.31) | collective-permute-done | bytes 262176 | tf_op jit(solution)/shard_map/ppermute | solution.py:293
  135.8 3.9 %march.62 = (f32[3,2000]{1,0:T(4,128)S(1)}, bf16[64,2048]{1,0:T(8,128)(2,1)S(1)}) custom-call(bf16[64,2048]{1,0:T(8,128)(2,1)S(1)} %collective-permute-done.31.incoming, bf16[3,2000,2000]{2,1,0:T(8,128)(2,1)S(1)} %bitcast.6, f32[3,64,2000]{2,1,0:T(8,128)S(1)} %get-tuple-element.73.cosine, ...), custom_call_target="tpu_custom_call", output_to_operand_aliasing={{0}: (6, {}), {1}: (0, {})} | custom-call | tf_op jit(solution)/shard_map/march/pallas_call | solution.py:261
  139.7 1.6 %collective-permute-done.30.incoming = bf16[64,2048]{1,0:T(8,128)(2,1)S(1)} collective-permute-done((bf16[64,2048]{1,0:T(8,128)(2,1)S(1)}, bf16[64,2048]{1,0:T(8,128)(2,1)S(1)}, u32[]{:S(2)}, u32[]{:S(2)}) %collective-permute-start.30) | collective-permute-done | bytes 262176 | tf_op jit(solution)/shard_map/ppermute | solution.py:293
  141.3 3.9 %march.63 = (f32[3,2000]{1,0:T(4,128)S(1)}, bf16[64,2048]{1,0:T(8,128)(2,1)S(1)}) custom-call(bf16[64,2048]{1,0:T(8,128)(2,1)S(1)} %collective-permute-done.30.incoming, bf16[3,2000,2000]{2,1,0:T(8,128)(2,1)S(1)} %bitcast.6, f32[3,64,2000]{2,1,0:T(8,128)S(1)} %get-tuple-element.73.cosine, ...), custom_call_target="tpu_custom_call", output_to_operand_aliasing={{0}: (6, {}), {1}: (0, {})} | custom-call | tf_op jit(solution)/shard_map/march/pallas_call | solution.py:261
  145.4 10.6 %all_to_all.5 = f32[8,3,250]{2,1,0:T(4,128)S(1)} all-to-all(f32[8,3,250]{2,1,0:T(4,128)S(1)} %bitcast.7), channel_id=1, replica_groups=mesh['stn'=16,'freq'=8] {'freq'}, dimensions={0} | all-to-all | bytes 48000 | tf_op jit(solution)/shard_map/all_to_all | solution.py:38
  (98 shorter events, 13.9 us)
Async XLA Ops:
  5.8 5.3 %collective-permute-start.1 = (bf16[2,64,2000]{2,1,0:T(8,128)(2,1)S(1)}, bf16[2,64,2000]{2,1,0:T(8,128)(2,1)S(1)}, u32[]{:S(2)}, u32[]{:S(2)}) collective-permute-start(bf16[2,64,2000]{2,1,0:T(8,128)(2,1)S(1)} %get-tuple-element.84), channel_id=1, source_target_pairs={{8,0},{24,16},{40,32},{56,48},{72,64},{88,80},{104,96},{120,112},{... | collective-permute-start | bytes 1536008 | tf_op jit(solution)/shard_map/ppermute | solution.py:27
  9.1 2.9 %collective-permute-start.2 = (bf16[64,2048]{1,0:T(8,128)(2,1)S(1)}, bf16[64,2048]{1,0:T(8,128)(2,1)S(1)}, u32[]{:S(2)}, u32[]{:S(2)}) collective-permute-start(bf16[64,2048]{1,0:T(8,128)(2,1)S(1)} %get-tuple-element.81), channel_id=1, source_target_pairs={{120,112},{121,113},{122,114},{123,115},{124,116},{125,117},{126,1... | collective-permute-start | bytes 786440 | tf_op jit(solution)/shard_map/ppermute | solution.py:293
  9.8 2.9 %collective-permute-start = (bf16[64,2048]{1,0:T(8,128)(2,1)S(1)}, bf16[64,2048]{1,0:T(8,128)(2,1)S(1)}, u32[]{:S(2)}, u32[]{:S(2)}) collective-permute-start(bf16[64,2048]{1,0:T(8,128)(2,1)S(1)} %get-tuple-element.78), channel_id=1, source_target_pairs={{120,112},{121,113},{122,114},{123,115},{124,116},{125,117},{126,1... | collective-permute-start | bytes 786440 | tf_op jit(solution)/shard_map/ppermute | solution.py:293
  10.5 2.9 %collective-permute-start.4 = (bf16[2,64,2000]{2,1,0:T(8,128)(2,1)S(1)}, bf16[2,64,2000]{2,1,0:T(8,128)(2,1)S(1)}, u32[]{:S(2)}, u32[]{:S(2)}) collective-permute-start(bf16[2,64,2000]{2,1,0:T(8,128)(2,1)S(1)} %get-tuple-element.84), channel_id=1, source_target_pairs={{16,8},{32,24},{48,40},{64,56},{80,72},{96,88},{112,104},{17,9},{3... | collective-permute-start | bytes 1536008 | tf_op jit(solution)/shard_map/ppermute | solution.py:27
  12.0 2.2 %collective-permute-start.5 = (bf16[64,2048]{1,0:T(8,128)(2,1)S(1)}, bf16[64,2048]{1,0:T(8,128)(2,1)S(1)}, u32[]{:S(2)}, u32[]{:S(2)}) collective-permute-start(bf16[64,2048]{1,0:T(8,128)(2,1)S(1)} %get-tuple-element.86), channel_id=1, source_target_pairs={{112,104},{113,105},{114,106},{115,107},{116,108},{117,109},{118,1... | collective-permute-start | bytes 786440 | tf_op jit(solution)/shard_map/ppermute | solution.py:293
  12.7 2.2 %collective-permute-start.3 = (bf16[64,2048]{1,0:T(8,128)(2,1)S(1)}, bf16[64,2048]{1,0:T(8,128)(2,1)S(1)}, u32[]{:S(2)}, u32[]{:S(2)}) collective-permute-start(bf16[64,2048]{1,0:T(8,128)(2,1)S(1)} %get-tuple-element.83), channel_id=1, source_target_pairs={{112,104},{113,105},{114,106},{115,107},{116,108},{117,109},{118,1... | collective-permute-start | bytes 786440 | tf_op jit(solution)/shard_map/ppermute | solution.py:293
  14.2 1.4 collective-permute-start.7
  15.0 1.4 collective-permute-start.6
  15.7 1.4 collective-permute-start.9
  16.4 1.4 collective-permute-start.8
  17.1 1.6 %collective-permute-start.11 = (bf16[64,2048]{1,0:T(8,128)(2,1)S(1)}, bf16[64,2048]{1,0:T(8,128)(2,1)S(1)}, u32[]{:S(2)}, u32[]{:S(2)}) collective-permute-start(bf16[64,2048]{1,0:T(8,128)(2,1)S(1)} %get-tuple-element.97), channel_id=1, source_target_pairs={{88,80},{89,81},{90,82},{91,83},{92,84},{93,85},{94,86},{95,87}} | collective-permute-start | bytes 786440 | tf_op jit(solution)/shard_map/ppermute | solution.py:293
  18.0 1.4 collective-permute-start.10
  18.7 1.4 collective-permute-start.13
  19.5 1.4 collective-permute-start.12
  20.2 1.4 collective-permute-start.15
  20.9 1.4 collective-permute-start.14
  21.6 1.4 collective-permute-start.17
  22.4 1.4 collective-permute-start.16
  23.1 1.4 collective-permute-start.19
  23.8 1.4 collective-permute-start.18
  30.3 1.6 %collective-permute-start.29 = (bf16[64,2048]{1,0:T(8,128)(2,1)S(1)}, bf16[64,2048]{1,0:T(8,128)(2,1)S(1)}, u32[]{:S(2)}, u32[]{:S(2)}) collective-permute-start(bf16[64,2048]{1,0:T(8,128)(2,1)S(1)} %get-tuple-element.133), channel_id=1, source_target_pairs={{16,8},{17,9},{18,10},{19,11},{20,12},{21,13},{22,14},{23,15}} | collective-permute-start | bytes 786440 | tf_op jit(solution)/shard_map/ppermute | solution.py:293
  31.2 2.0 %collective-permute-start.28 = (bf16[64,2048]{1,0:T(8,128)(2,1)S(1)}, bf16[64,2048]{1,0:T(8,128)(2,1)S(1)}, u32[]{:S(2)}, u32[]{:S(2)}) collective-permute-start(bf16[64,2048]{1,0:T(8,128)(2,1)S(1)} %get-tuple-element.132), channel_id=1, source_target_pairs={{16,8},{17,9},{18,10},{19,11},{20,12},{21,13},{22,14},{23,15}} | collective-permute-start | bytes 786440 | tf_op jit(solution)/shard_map/ppermute | solution.py:293
  32.0 103.9 %collective-permute-start.31 = (bf16[64,2048]{1,0:T(8,128)(2,1)S(1)}, bf16[64,2048]{1,0:T(8,128)(2,1)S(1)}, u32[]{:S(2)}, u32[]{:S(2)}) collective-permute-start(bf16[64,2048]{1,0:T(8,128)(2,1)S(1)} %get-tuple-element.137), channel_id=1, source_target_pairs={{8,0},{9,1},{10,2},{11,3},{12,4},{13,5},{14,6},{15,7}} | collective-permute-start | bytes 786440 | tf_op jit(solution)/shard_map/ppermute | solution.py:293
  33.3 108.0 %collective-permute-start.30 = (bf16[64,2048]{1,0:T(8,128)(2,1)S(1)}, bf16[64,2048]{1,0:T(8,128)(2,1)S(1)}, u32[]{:S(2)}, u32[]{:S(2)}) collective-permute-start(bf16[64,2048]{1,0:T(8,128)(2,1)S(1)} %get-tuple-element.136), channel_id=1, source_target_pairs={{8,0},{9,1},{10,2},{11,3},{12,4},{13,5},{14,6},{15,7}} | collective-permute-start | bytes 786440 | tf_op jit(solution)/shard_map/ppermute | solution.py:293
  (15 other events, 59.6 us)

commit v4 on v3

--- a/solution.py
+++ b/solution.py
@@ -232,13 +232,23 @@
 
             push(0, 0)
             lax.fori_loop(0, full - 1, deepen, 0)
-            deepen(full - 1, 0)
-            state = state_at(full)
-            for group in range(groups):
-                if group + 1 < groups:
-                    push(full, group + 1)
-                accumulate(state, group)
-            for tile in range(tiles):
+            states = [state_at(full - 1), state_at(full)]
+            order = [(late, group) for group in range(groups) for late in range(2)]
+
+            def push_late(turn):
+                late, group = order[turn]
+                for unit in range(UNITS):
+                    pltpu.matmul_push_rhs(piece(full - 1 + late, UNITS * group + unit), turn % 2, unit)
+
+            for turn, (late, group) in enumerate(order):
+                if turn + 1 < len(order):
+                    push_late(turn + 1)
+                for unit in range(UNITS):
+                    pltpu.matmul_acc_lhs(sums_of[UNITS * group + unit], states[late], load_staged_rhs=turn % 2)
+                if late == 0 and group > 0:
+                    for tile in range(UNITS * (group - 1), UNITS * group):
+                        settle(station, tile, pltpu.matmul_pop(sums_of[tile]))
+            for tile in range(UNITS * (groups - 1), tiles):
                 settle(station, tile, pltpu.matmul_pop(sums_of[tile]))
             return carried
 

time: 157 us -> 158 us (level)
  no operation moved by 1% of the time
where the time goes in v4:
time: 158 us
  waiting for transfers between devices  104 us (66%)
  starting transfers between devices  23.8 us (15%)
  Pallas kernels  16.3 us (10%)
  blocking collectives  10.6 us (7%)
  local copies, waits for them, and re-layouts  1.74 us (1%)
    ppermute x30, waiting for transfers between devices, body(): outgoing.append(lax.ppermute(out, 'stn', [(here, here - 1)]))  104 us
    ppermute x30, starting transfers between devices, body(): outgoing.append(lax.ppermute(out, 'stn', [(here, here - 1)]))  21.5 us
    all_to_all x1, blocking collectives, summed_on_arrival(): lax.all_to_all(in_blocks(value, dim, length), axis, 0, 0, tiled=True)  10.6 us
    pallas_call x32, Pallas kernels, march(): pl.pallas_call(functools.partial(march_kernel, turn, block, first), out_s...  8.93 us
    pallas_call x1, Pallas kernels, prepare(): pl.pallas_call(prepare_kernel, out_shape=(pltpu.VMEM((stations, freqs, wi...  5.81 us
  transfers between devices with their start and end apart: 32, of which 2 were waited for; matrix products, arithmetic and copies ran while one was open for 0% of the time, Pallas kernels for 4%

profile of v4, /device:TPU:0, one launch (start us, length us, event | category | flops | bytes accessed | tf_op | source)
XLA Modules:
  0.0 158.0 jit_solution(14370112143773642533)
XLA Ops:
  0.0 5.8 %prepare.1 = (f32[3,64,2000]{2,1,0:T(8,128)S(1)}, f32[3,64,2000]{2,1,0:T(8,128)S(1)}, f32[3,2,64,2000]{3,2,1,0:T(8,128)S(1)}, bf16[2,64,2000]{2,1,0:T(8,128)(2,1)S(1)}, f32[3,2,64,2000]{3,2,1,0:T(8,128)S(1)}) custom-call(s32[3]{0:T(128)} %gap.3, s32[64]{0:T(128)} %freq_index_hbm.1, bf16[3,2,64,2000]{3,2,1,0:T(8,128)(2,1)} %forward_hbm.1, f32[1,2000]{1,0:T(1,128)} %bitcast.8, ...), custom_call_target="tpu_custom_call" | custom-call | flops 17179869184 | bytes 67108864 | tf_op jit(solution)/shard_map/prepare/pallas_call | solution.py:106
  5.8 1.6 collective-permute-start.1
  8.0 1.0 slice-done.5
  9.8 0.7 collective-permute-start
  10.5 0.7 collective-permute-start.4
  11.2 0.8 finish.2.slope.slope_in
  12.7 0.7 collective-permute-start.3
  13.4 0.8 finish.3.slope
  15.0 0.7 collective-permute-start.6
  17.1 0.7 collective-permute-start.11
  19.5 0.7 collective-permute-start.12
  20.2 0.7 collective-permute-start.15
  22.4 0.7 collective-permute-start.16
  25.2 0.7 collective-permute-start.20
  27.4 0.7 collective-permute-start.25
  28.1 0.7 collective-permute-start.24
  30.3 0.7 collective-permute-start.29
  32.0 1.3 collective-permute-start.31
  33.3 1.3 collective-permute-start.30
  34.6 102.5 %collective-permute-done.31.incoming = bf16[64,2048]{1,0:T(8,128)(2,1)S(1)} collective-permute-done((bf16[64,2048]{1,0:T(8,128)(2,1)S(1)}, bf16[64,2048]{1,0:T(8,128)(2,1)S(1)}, u32[]{:S(2)}, u32[]{:S(2)}) %collective-permute-start.31) | collective-permute-done | bytes 262176 | tf_op jit(solution)/shard_map/ppermute | solution.py:303
  137.1 4.0 %march.62 = (f32[3,2000]{1,0:T(4,128)S(1)}, bf16[64,2048]{1,0:T(8,128)(2,1)S(1)}) custom-call(bf16[64,2048]{1,0:T(8,128)(2,1)S(1)} %collective-permute-done.31.incoming, bf16[3,2000,2000]{2,1,0:T(8,128)(2,1)S(1)} %bitcast.6, f32[3,64,2000]{2,1,0:T(8,128)S(1)} %get-tuple-element.73.cosine, ...), custom_call_target="tpu_custom_call", output_to_operand_aliasing={{0}: (6, {}), {1}: (0, {})} | custom-call | tf_op jit(solution)/shard_map/march/pallas_call | solution.py:271
  141.1 1.6 collective-permute-done.30.incoming
  142.7 4.0 %march.63 = (f32[3,2000]{1,0:T(4,128)S(1)}, bf16[64,2048]{1,0:T(8,128)(2,1)S(1)}) custom-call(bf16[64,2048]{1,0:T(8,128)(2,1)S(1)} %collective-permute-done.30.incoming, bf16[3,2000,2000]{2,1,0:T(8,128)(2,1)S(1)} %bitcast.6, f32[3,64,2000]{2,1,0:T(8,128)S(1)} %get-tuple-element.73.cosine, ...), custom_call_target="tpu_custom_call", output_to_operand_aliasing={{0}: (6, {}), {1}: (0, {})} | custom-call | tf_op jit(solution)/shard_map/march/pallas_call | solution.py:271
  146.8 10.6 %all_to_all.5 = f32[8,3,250]{2,1,0:T(4,128)S(1)} all-to-all(f32[8,3,250]{2,1,0:T(4,128)S(1)} %bitcast.7), channel_id=1, replica_groups=mesh['stn'=16,'freq'=8] {'freq'}, dimensions={0} | all-to-all | bytes 48000 | tf_op jit(solution)/shard_map/all_to_all | solution.py:38
  (98 shorter events, 13.9 us)
Async XLA Ops:
  5.8 5.3 %collective-permute-start.1 = (bf16[2,64,2000]{2,1,0:T(8,128)(2,1)S(1)}, bf16[2,64,2000]{2,1,0:T(8,128)(2,1)S(1)}, u32[]{:S(2)}, u32[]{:S(2)}) collective-permute-start(bf16[2,64,2000]{2,1,0:T(8,128)(2,1)S(1)} %get-tuple-element.84), channel_id=1, source_target_pairs={{8,0},{24,16},{40,32},{56,48},{72,64},{88,80},{104,96},{120,112},{... | collective-permute-start | bytes 1536008 | tf_op jit(solution)/shard_map/ppermute | solution.py:27
  9.1 2.9 %collective-permute-start.2 = (bf16[64,2048]{1,0:T(8,128)(2,1)S(1)}, bf16[64,2048]{1,0:T(8,128)(2,1)S(1)}, u32[]{:S(2)}, u32[]{:S(2)}) collective-permute-start(bf16[64,2048]{1,0:T(8,128)(2,1)S(1)} %get-tuple-element.81), channel_id=1, source_target_pairs={{120,112},{121,113},{122,114},{123,115},{124,116},{125,117},{126,1... | collective-permute-start | bytes 786440 | tf_op jit(solution)/shard_map/ppermute | solution.py:303
  9.8 2.9 %collective-permute-start = (bf16[64,2048]{1,0:T(8,128)(2,1)S(1)}, bf16[64,2048]{1,0:T(8,128)(2,1)S(1)}, u32[]{:S(2)}, u32[]{:S(2)}) collective-permute-start(bf16[64,2048]{1,0:T(8,128)(2,1)S(1)} %get-tuple-element.78), channel_id=1, source_target_pairs={{120,112},{121,113},{122,114},{123,115},{124,116},{125,117},{126,1... | collective-permute-start | bytes 786440 | tf_op jit(solution)/shard_map/ppermute | solution.py:303
  10.5 2.9 %collective-permute-start.4 = (bf16[2,64,2000]{2,1,0:T(8,128)(2,1)S(1)}, bf16[2,64,2000]{2,1,0:T(8,128)(2,1)S(1)}, u32[]{:S(2)}, u32[]{:S(2)}) collective-permute-start(bf16[2,64,2000]{2,1,0:T(8,128)(2,1)S(1)} %get-tuple-element.84), channel_id=1, source_target_pairs={{16,8},{32,24},{48,40},{64,56},{80,72},{96,88},{112,104},{17,9},{3... | collective-permute-start | bytes 1536008 | tf_op jit(solution)/shard_map/ppermute | solution.py:27
  12.0 2.2 %collective-permute-start.5 = (bf16[64,2048]{1,0:T(8,128)(2,1)S(1)}, bf16[64,2048]{1,0:T(8,128)(2,1)S(1)}, u32[]{:S(2)}, u32[]{:S(2)}) collective-permute-start(bf16[64,2048]{1,0:T(8,128)(2,1)S(1)} %get-tuple-element.86), channel_id=1, source_target_pairs={{112,104},{113,105},{114,106},{115,107},{116,108},{117,109},{118,1... | collective-permute-start | bytes 786440 | tf_op jit(solution)/shard_map/ppermute | solution.py:303
  12.7 2.2 %collective-permute-start.3 = (bf16[64,2048]{1,0:T(8,128)(2,1)S(1)}, bf16[64,2048]{1,0:T(8,128)(2,1)S(1)}, u32[]{:S(2)}, u32[]{:S(2)}) collective-permute-start(bf16[64,2048]{1,0:T(8,128)(2,1)S(1)} %get-tuple-element.83), channel_id=1, source_target_pairs={{112,104},{113,105},{114,106},{115,107},{116,108},{117,109},{118,1... | collective-permute-start | bytes 786440 | tf_op jit(solution)/shard_map/ppermute | solution.py:303
  14.2 1.4 collective-permute-start.7
  15.0 1.4 collective-permute-start.6
  15.7 1.4 collective-permute-start.9
  16.4 1.4 collective-permute-start.8
  17.1 1.6 %collective-permute-start.11 = (bf16[64,2048]{1,0:T(8,128)(2,1)S(1)}, bf16[64,2048]{1,0:T(8,128)(2,1)S(1)}, u32[]{:S(2)}, u32[]{:S(2)}) collective-permute-start(bf16[64,2048]{1,0:T(8,128)(2,1)S(1)} %get-tuple-element.97), channel_id=1, source_target_pairs={{88,80},{89,81},{90,82},{91,83},{92,84},{93,85},{94,86},{95,87}} | collective-permute-start | bytes 786440 | tf_op jit(solution)/shard_map/ppermute | solution.py:303
  18.0 1.4 collective-permute-start.10
  18.7 1.4 collective-permute-start.13
  19.5 1.4 collective-permute-start.12
  20.2 1.4 collective-permute-start.15
  20.9 1.4 collective-permute-start.14
  21.6 1.4 collective-permute-start.17
  22.4 1.4 collective-permute-start.16
  23.1 1.4 collective-permute-start.19
  23.8 1.4 collective-permute-start.18
  30.3 1.6 %collective-permute-start.29 = (bf16[64,2048]{1,0:T(8,128)(2,1)S(1)}, bf16[64,2048]{1,0:T(8,128)(2,1)S(1)}, u32[]{:S(2)}, u32[]{:S(2)}) collective-permute-start(bf16[64,2048]{1,0:T(8,128)(2,1)S(1)} %get-tuple-element.133), channel_id=1, source_target_pairs={{16,8},{17,9},{18,10},{19,11},{20,12},{21,13},{22,14},{23,15}} | collective-permute-start | bytes 786440 | tf_op jit(solution)/shard_map/ppermute | solution.py:303
  31.2 2.0 %collective-permute-start.28 = (bf16[64,2048]{1,0:T(8,128)(2,1)S(1)}, bf16[64,2048]{1,0:T(8,128)(2,1)S(1)}, u32[]{:S(2)}, u32[]{:S(2)}) collective-permute-start(bf16[64,2048]{1,0:T(8,128)(2,1)S(1)} %get-tuple-element.132), channel_id=1, source_target_pairs={{16,8},{17,9},{18,10},{19,11},{20,12},{21,13},{22,14},{23,15}} | collective-permute-start | bytes 786440 | tf_op jit(solution)/shard_map/ppermute | solution.py:303
  32.0 105.2 %collective-permute-start.31 = (bf16[64,2048]{1,0:T(8,128)(2,1)S(1)}, bf16[64,2048]{1,0:T(8,128)(2,1)S(1)}, u32[]{:S(2)}, u32[]{:S(2)}) collective-permute-start(bf16[64,2048]{1,0:T(8,128)(2,1)S(1)} %get-tuple-element.137), channel_id=1, source_target_pairs={{8,0},{9,1},{10,2},{11,3},{12,4},{13,5},{14,6},{15,7}} | collective-permute-start | bytes 786440 | tf_op jit(solution)/shard_map/ppermute | solution.py:303
  33.3 109.4 %collective-permute-start.30 = (bf16[64,2048]{1,0:T(8,128)(2,1)S(1)}, bf16[64,2048]{1,0:T(8,128)(2,1)S(1)}, u32[]{:S(2)}, u32[]{:S(2)}) collective-permute-start(bf16[64,2048]{1,0:T(8,128)(2,1)S(1)} %get-tuple-element.136), channel_id=1, source_target_pairs={{8,0},{9,1},{10,2},{11,3},{12,4},{13,5},{14,6},{15,7}} | collective-permute-start | bytes 786440 | tf_op jit(solution)/shard_map/ppermute | solution.py:303
  (15 other events, 59.6 us)

commit v5 on v3

--- a/solution.py
+++ b/solution.py
@@ -231,7 +231,15 @@
                 return carried
 
             push(0, 0)
-            lax.fori_loop(0, full - 1, deepen, 0)
+            def deepen_twice(step, carried):
+                return deepen(2 * step + 1, deepen(2 * step, carried))
+
+            if block == 0:
+                lax.fori_loop(0, (full - 1) // 2, deepen_twice, 0)
+                if (full - 1) % 2:
+                    deepen(full - 2, 0)
+            else:
+                lax.fori_loop(0, full - 1, deepen, 0)
             deepen(full - 1, 0)
             state = state_at(full)
             for group in range(groups):

time: 157 us -> 157 us (level)
  no operation moved by 1% of the time
where the time goes in v5:
time: 157 us
  waiting for transfers between devices  103 us (66%)
  starting transfers between devices  23.8 us (15%)
  Pallas kernels  16.1 us (10%)
  blocking collectives  10.5 us (7%)
  local copies, waits for them, and re-layouts  1.74 us (1%)
    ppermute x30, waiting for transfers between devices, body(): outgoing.append(lax.ppermute(out, 'stn', [(here, here - 1)]))  103 us
    ppermute x30, starting transfers between devices, body(): outgoing.append(lax.ppermute(out, 'stn', [(here, here - 1)]))  21.5 us
    all_to_all x1, blocking collectives, summed_on_arrival(): lax.all_to_all(in_blocks(value, dim, length), axis, 0, 0, tiled=True)  10.5 us
    pallas_call x32, Pallas kernels, march(): pl.pallas_call(functools.partial(march_kernel, turn, block, first), out_s...  8.79 us
    pallas_call x1, Pallas kernels, prepare(): pl.pallas_call(prepare_kernel, out_shape=(pltpu.VMEM((stations, freqs, wi...  5.81 us
  transfers between devices with their start and end apart: 32, of which 2 were waited for; matrix products, arithmetic and copies ran while one was open for 0% of the time, Pallas kernels for 4%

profile of v5, /device:TPU:0, one launch (start us, length us, event | category | flops | bytes accessed | tf_op | source)
XLA Modules:
  0.0 156.8 jit_solution(6019932095959482805)
XLA Ops:
  0.0 5.8 %prepare.1 = (f32[3,64,2000]{2,1,0:T(8,128)S(1)}, f32[3,64,2000]{2,1,0:T(8,128)S(1)}, f32[3,2,64,2000]{3,2,1,0:T(8,128)S(1)}, bf16[2,64,2000]{2,1,0:T(8,128)(2,1)S(1)}, f32[3,2,64,2000]{3,2,1,0:T(8,128)S(1)}) custom-call(s32[3]{0:T(128)} %gap.3, s32[64]{0:T(128)} %freq_index_hbm.1, bf16[3,2,64,2000]{3,2,1,0:T(8,128)(2,1)} %forward_hbm.1, f32[1,2000]{1,0:T(1,128)} %bitcast.8, ...), custom_call_target="tpu_custom_call" | custom-call | flops 17179869184 | bytes 67108864 | tf_op jit(solution)/shard_map/prepare/pallas_call | solution.py:106
  5.8 1.6 collective-permute-start.1
  8.0 1.0 slice-done.5
  10.5 0.7 collective-permute-start.4
  11.2 0.8 finish.2.slope.slope_in
  12.7 0.7 collective-permute-start.3
  13.4 0.8 finish.3.slope
  15.0 0.7 collective-permute-start.6
  17.3 0.7 collective-permute-start.11
  19.5 0.7 collective-permute-start.12
  20.2 0.7 collective-permute-start.15
  22.4 0.7 collective-permute-start.16
  25.2 0.7 collective-permute-start.20
  27.4 0.7 collective-permute-start.25
  28.1 0.7 collective-permute-start.24
  29.8 0.7 collective-permute-start.26
  30.5 0.7 collective-permute-start.29
  32.0 1.3 collective-permute-start.31
  33.3 1.3 collective-permute-start.30
  34.6 101.8 %collective-permute-done.31.incoming = bf16[64,2048]{1,0:T(8,128)(2,1)S(1)} collective-permute-done((bf16[64,2048]{1,0:T(8,128)(2,1)S(1)}, bf16[64,2048]{1,0:T(8,128)(2,1)S(1)}, u32[]{:S(2)}, u32[]{:S(2)}) %collective-permute-start.31) | collective-permute-done | bytes 262176 | tf_op jit(solution)/shard_map/ppermute | solution.py:301
  136.4 3.9 %march.62 = (f32[3,2000]{1,0:T(4,128)S(1)}, bf16[64,2048]{1,0:T(8,128)(2,1)S(1)}) custom-call(bf16[64,2048]{1,0:T(8,128)(2,1)S(1)} %collective-permute-done.31.incoming, bf16[3,2000,2000]{2,1,0:T(8,128)(2,1)S(1)} %bitcast.6, f32[3,64,2000]{2,1,0:T(8,128)S(1)} %get-tuple-element.73.cosine, ...), custom_call_target="tpu_custom_call", output_to_operand_aliasing={{0}: (6, {}), {1}: (0, {})} | custom-call | tf_op jit(solution)/shard_map/march/pallas_call | solution.py:269
  140.3 1.3 collective-permute-done.30.incoming
  141.6 3.9 %march.63 = (f32[3,2000]{1,0:T(4,128)S(1)}, bf16[64,2048]{1,0:T(8,128)(2,1)S(1)}) custom-call(bf16[64,2048]{1,0:T(8,128)(2,1)S(1)} %collective-permute-done.30.incoming, bf16[3,2000,2000]{2,1,0:T(8,128)(2,1)S(1)} %bitcast.6, f32[3,64,2000]{2,1,0:T(8,128)S(1)} %get-tuple-element.73.cosine, ...), custom_call_target="tpu_custom_call", output_to_operand_aliasing={{0}: (6, {}), {1}: (0, {})} | custom-call | tf_op jit(solution)/shard_map/march/pallas_call | solution.py:269
  145.7 10.5 %all_to_all.5 = f32[8,3,250]{2,1,0:T(4,128)S(1)} all-to-all(f32[8,3,250]{2,1,0:T(4,128)S(1)} %bitcast.7), channel_id=1, replica_groups=mesh['stn'=16,'freq'=8] {'freq'}, dimensions={0} | all-to-all | bytes 48000 | tf_op jit(solution)/shard_map/all_to_all | solution.py:38
  (98 shorter events, 13.9 us)
Async XLA Ops:
  5.8 5.3 %collective-permute-start.1 = (bf16[2,64,2000]{2,1,0:T(8,128)(2,1)S(1)}, bf16[2,64,2000]{2,1,0:T(8,128)(2,1)S(1)}, u32[]{:S(2)}, u32[]{:S(2)}) collective-permute-start(bf16[2,64,2000]{2,1,0:T(8,128)(2,1)S(1)} %get-tuple-element.84), channel_id=1, source_target_pairs={{8,0},{24,16},{40,32},{56,48},{72,64},{88,80},{104,96},{120,112},{... | collective-permute-start | bytes 1536008 | tf_op jit(solution)/shard_map/ppermute | solution.py:27
  9.1 2.9 %collective-permute-start.2 = (bf16[64,2048]{1,0:T(8,128)(2,1)S(1)}, bf16[64,2048]{1,0:T(8,128)(2,1)S(1)}, u32[]{:S(2)}, u32[]{:S(2)}) collective-permute-start(bf16[64,2048]{1,0:T(8,128)(2,1)S(1)} %get-tuple-element.81), channel_id=1, source_target_pairs={{120,112},{121,113},{122,114},{123,115},{124,116},{125,117},{126,1... | collective-permute-start | bytes 786440 | tf_op jit(solution)/shard_map/ppermute | solution.py:301
  9.8 2.9 %collective-permute-start = (bf16[64,2048]{1,0:T(8,128)(2,1)S(1)}, bf16[64,2048]{1,0:T(8,128)(2,1)S(1)}, u32[]{:S(2)}, u32[]{:S(2)}) collective-permute-start(bf16[64,2048]{1,0:T(8,128)(2,1)S(1)} %get-tuple-element.78), channel_id=1, source_target_pairs={{120,112},{121,113},{122,114},{123,115},{124,116},{125,117},{126,1... | collective-permute-start | bytes 786440 | tf_op jit(solution)/shard_map/ppermute | solution.py:301
  10.5 2.9 %collective-permute-start.4 = (bf16[2,64,2000]{2,1,0:T(8,128)(2,1)S(1)}, bf16[2,64,2000]{2,1,0:T(8,128)(2,1)S(1)}, u32[]{:S(2)}, u32[]{:S(2)}) collective-permute-start(bf16[2,64,2000]{2,1,0:T(8,128)(2,1)S(1)} %get-tuple-element.84), channel_id=1, source_target_pairs={{16,8},{32,24},{48,40},{64,56},{80,72},{96,88},{112,104},{17,9},{3... | collective-permute-start | bytes 1536008 | tf_op jit(solution)/shard_map/ppermute | solution.py:27
  12.0 2.2 %collective-permute-start.5 = (bf16[64,2048]{1,0:T(8,128)(2,1)S(1)}, bf16[64,2048]{1,0:T(8,128)(2,1)S(1)}, u32[]{:S(2)}, u32[]{:S(2)}) collective-permute-start(bf16[64,2048]{1,0:T(8,128)(2,1)S(1)} %get-tuple-element.86), channel_id=1, source_target_pairs={{112,104},{113,105},{114,106},{115,107},{116,108},{117,109},{118,1... | collective-permute-start | bytes 786440 | tf_op jit(solution)/shard_map/ppermute | solution.py:301
  12.7 2.2 %collective-permute-start.3 = (bf16[64,2048]{1,0:T(8,128)(2,1)S(1)}, bf16[64,2048]{1,0:T(8,128)(2,1)S(1)}, u32[]{:S(2)}, u32[]{:S(2)}) collective-permute-start(bf16[64,2048]{1,0:T(8,128)(2,1)S(1)} %get-tuple-element.83), channel_id=1, source_target_pairs={{112,104},{113,105},{114,106},{115,107},{116,108},{117,109},{118,1... | collective-permute-start | bytes 786440 | tf_op jit(solution)/shard_map/ppermute | solution.py:301
  14.2 1.4 collective-permute-start.7
  15.0 1.4 collective-permute-start.6
  15.7 1.4 collective-permute-start.9
  16.4 1.6 %collective-permute-start.8 = (bf16[64,2048]{1,0:T(8,128)(2,1)S(1)}, bf16[64,2048]{1,0:T(8,128)(2,1)S(1)}, u32[]{:S(2)}, u32[]{:S(2)}) collective-permute-start(bf16[64,2048]{1,0:T(8,128)(2,1)S(1)} %get-tuple-element.92), channel_id=1, source_target_pairs={{96,88},{97,89},{98,90},{99,91},{100,92},{101,93},{102,94},{103,95}} | collective-permute-start | bytes 786440 | tf_op jit(solution)/shard_map/ppermute | solution.py:301
  17.3 1.4 collective-permute-start.11
  18.0 1.4 collective-permute-start.10
  18.7 1.4 collective-permute-start.13
  19.5 1.4 collective-permute-start.12
  20.2 1.4 collective-permute-start.15
  20.9 1.4 collective-permute-start.14
  21.6 1.4 collective-permute-start.17
  22.4 1.4 collective-permute-start.16
  23.1 1.4 collective-permute-start.19
  23.8 1.4 collective-permute-start.18
  28.1 1.6 %collective-permute-start.24 = (bf16[64,2048]{1,0:T(8,128)(2,1)S(1)}, bf16[64,2048]{1,0:T(8,128)(2,1)S(1)}, u32[]{:S(2)}, u32[]{:S(2)}) collective-permute-start(bf16[64,2048]{1,0:T(8,128)(2,1)S(1)} %get-tuple-element.124), channel_id=1, source_target_pairs={{32,24},{33,25},{34,26},{35,27},{36,28},{37,29},{38,30},{39,31}} | collective-permute-start | bytes 786440 | tf_op jit(solution)/shard_map/ppermute | solution.py:301
  31.2 2.0 %collective-permute-start.28 = (bf16[64,2048]{1,0:T(8,128)(2,1)S(1)}, bf16[64,2048]{1,0:T(8,128)(2,1)S(1)}, u32[]{:S(2)}, u32[]{:S(2)}) collective-permute-start(bf16[64,2048]{1,0:T(8,128)(2,1)S(1)} %get-tuple-element.132), channel_id=1, source_target_pairs={{16,8},{17,9},{18,10},{19,11},{20,12},{21,13},{22,14},{23,15}} | collective-permute-start | bytes 786440 | tf_op jit(solution)/shard_map/ppermute | solution.py:301
  32.0 104.4 %collective-permute-start.31 = (bf16[64,2048]{1,0:T(8,128)(2,1)S(1)}, bf16[64,2048]{1,0:T(8,128)(2,1)S(1)}, u32[]{:S(2)}, u32[]{:S(2)}) collective-permute-start(bf16[64,2048]{1,0:T(8,128)(2,1)S(1)} %get-tuple-element.137), channel_id=1, source_target_pairs={{8,0},{9,1},{10,2},{11,3},{12,4},{13,5},{14,6},{15,7}} | collective-permute-start | bytes 786440 | tf_op jit(solution)/shard_map/ppermute | solution.py:301
  33.3 108.3 %collective-permute-start.30 = (bf16[64,2048]{1,0:T(8,128)(2,1)S(1)}, bf16[64,2048]{1,0:T(8,128)(2,1)S(1)}, u32[]{:S(2)}, u32[]{:S(2)}) collective-permute-start(bf16[64,2048]{1,0:T(8,128)(2,1)S(1)} %get-tuple-element.136), channel_id=1, source_target_pairs={{8,0},{9,1},{10,2},{11,3},{12,4},{13,5},{14,6},{15,7}} | collective-permute-start | bytes 786440 | tf_op jit(solution)/shard_map/ppermute | solution.py:301
  (15 other events, 59.6 us)
